TPU v7x, 128 devices: a whole 4x4x4 slice. The times are simulated.
128 devices in a mesh: row: 16 (over x, y), col: 8 (over z, core).
Axes of the slice: x: 4, y: 4, z: 4, core: 2. Of those that a mesh axis runs over, the one named last changes fastest.
Arguments:
- child_tiles: float32 [14336, 256, 128], P(('row', 'col')), may hold values from -2.5 to 2.5
- tile_dest: int32 [14336], P(('row', 'col')), may hold values from 0 to 6143, as said below
- tile_mask: int32 [14336, 256], P(('row', 'col')), may hold values 0 or 1
- tile_count: int32 [128], P(('row', 'col')), may hold values from 84 to 112, as said below
- front_diagonal: float32 [2, 2048], P(None, 'col'), may hold values from 200 to 400
Outputs:
- front_out: float32 [49152, 2, 2048], P('row', None, 'col')
Inputs may be any that keep to these rules, and one draw needn't show every extreme that they name: tile_dest[i] = r * 32 + t names front rows r * 256 onward and slab columns t * 128 onward; of the 112 tiles of one device at most 2 name tiles that lie on any one device of front_out's placement, and that most is reached. Tile i * 112 + m is live when m < tile_count[i].
All inputs are finite; a program needn't handle non-finite values. No bound on the sum of `tile_mask` on one device may be relied on, other than what follows from the above.
Results may differ from a plain program's by a relative error of at most 0.0001.
Values sent between devices are 32-bit elements; how exact they have to be, the bound alone decides.
No kernel may reach another device: no remote copies, remote signals or barrier semaphores. Data moves between devices by JAX's collectives and lax.ppermute only.
A program may use at most 192 MiB of HBM per device.

v0:
```python
import jax
import jax.numpy as jnp
from jax import lax
from jax.sharding import PartitionSpec as P

NF = 49152
CAP = 2


def from_root(x, axis, root):
    mine = lax.axis_index(axis) == root
    return lax.psum(jnp.where(mine, x, jnp.zeros_like(x)), axis)


def factor_panel(front_local, section, rows_global, cols_global, row_index, col_index):
    local_rows, col_blocks, panel_width = front_local.shape
    n_col = lax.axis_size("col")
    lower_edge = section * panel_width
    upper_edge = lower_edge + panel_width
    owner_col = section % n_col
    owner_block = section // n_col
    owner_row = lower_edge // local_rows
    start_row = lower_edge - owner_row * local_rows
    column = front_local[:, owner_block, :]
    diag_piece = lax.slice_in_dim(column, start_row, start_row + panel_width, axis=0)
    is_root = jnp.logical_and(row_index == owner_row, col_index == owner_col)
    diag_piece = jnp.where(is_root, diag_piece, jnp.eye(panel_width, dtype=jnp.float32))
    pivot = from_root(diag_piece, ("row", "col"), owner_row * n_col + owner_col)
    factor = jnp.linalg.cholesky(0.5 * (pivot + pivot.T))
    panel_raw = from_root(column, "col", owner_col)
    solved = jax.scipy.linalg.solve_triangular(factor, panel_raw.T, lower=True).T
    inner_row = jnp.clip(rows_global - lower_edge, 0, panel_width - 1)
    factor_rows = factor[inner_row]
    row_column = rows_global[:, None]
    lower_panel = jnp.where(
        row_column < lower_edge,
        jnp.zeros_like(solved),
        jnp.where(row_column < upper_edge, factor_rows, solved),
    )
    offset = cols_global - row_index * local_rows
    inside = jnp.logical_and(offset >= 0, offset < local_rows)
    picked = lower_panel[jnp.clip(offset, 0, local_rows - 1)] * inside[:, :, None].astype(
        jnp.float32
    )
    panel_rows = lax.psum(picked, "row")
    return (lower_panel, panel_rows)


def advance(front_part, lower_panel, panel_rows, section, cols_part):
    local_rows, col_blocks, panel_width = front_part.shape
    product = jnp.dot(
        lower_panel, panel_rows.reshape(-1, panel_width).T, precision=lax.Precision.HIGHEST
    ).reshape(local_rows, col_blocks, panel_width)
    upper_edge = (section + 1) * panel_width
    trailing = (cols_part >= upper_edge)[None, :, :]
    own_block = (cols_part // panel_width == section)[None, :, :]
    return jnp.where(
        trailing, front_part - product, jnp.where(own_block, lower_panel[:, None, :], front_part)
    )


def on_device(child_tiles, tile_dest, tile_mask, tile_count, front_diagonal):
    n_row = lax.axis_size("row")
    n_col = lax.axis_size("col")
    devices = n_row * n_col
    row_index = lax.axis_index("row")
    col_index = lax.axis_index("col")
    tile_total, tile_rows, tile_cols = child_tiles.shape
    col_blocks, panel_width = front_diagonal.shape
    halves = panel_width // tile_cols
    local_rows = NF // n_row
    row_tiles = local_rows // tile_rows
    col_tiles = col_blocks * n_col * halves
    is_live = jnp.arange(tile_total, dtype=jnp.int32) < tile_count[0]
    row_tile = tile_dest // col_tiles
    col_tile = tile_dest % col_tiles
    col_block = col_tile // halves
    col_half = col_tile % halves
    owner_row = row_tile // row_tiles
    owner_dev = jnp.where(is_live, owner_row * n_col + col_block % n_col, devices)
    onehot = (owner_dev[:, None] == jnp.arange(devices, dtype=jnp.int32)[None, :]).astype(jnp.int32)
    slot_rank = jnp.sum((jnp.cumsum(onehot, axis=0) - onehot) * onehot, axis=1)
    position = jnp.where(is_live, owner_dev * CAP + slot_rank, devices * CAP)
    local_tile = (
        (row_tile - owner_row * row_tiles) * (col_blocks * halves)
        + col_block // n_col * halves
        + col_half
    )
    masked = child_tiles * tile_mask.astype(jnp.float32)[:, :, None]
    outgoing = (
        jnp.zeros((devices * CAP + 1, tile_rows, tile_cols), jnp.float32)
        .at[position]
        .set(masked)[: devices * CAP]
    )
    targets = (
        jnp.full((devices * CAP + 1,), -1, jnp.int32).at[position].set(local_tile)[: devices * CAP]
    )
    arrived, arrived_targets = (
        lax.all_to_all(
            outgoing.reshape(devices, CAP, tile_rows, tile_cols),
            ("row", "col"),
            split_axis=0,
            concat_axis=0,
            tiled=True,
        ),
        lax.all_to_all(
            targets.reshape(devices, CAP), ("row", "col"), split_axis=0, concat_axis=0, tiled=True
        ),
    )
    n_local = row_tiles * col_blocks * halves
    flat_targets = arrived_targets.reshape(-1)
    flat_targets = jnp.where(flat_targets < 0, n_local, flat_targets)
    summed = jax.ops.segment_sum(
        arrived.reshape(-1, tile_rows, tile_cols), flat_targets, num_segments=n_local + 1
    )[:n_local]
    front_local = summed.reshape(row_tiles, col_blocks, halves, tile_rows, tile_cols)
    front_local = front_local.transpose(0, 3, 1, 2, 4).reshape(local_rows, col_blocks, panel_width)
    cols_global = (
        jnp.arange(col_blocks, dtype=jnp.int32)[:, None] * n_col + col_index
    ) * panel_width + jnp.arange(panel_width, dtype=jnp.int32)[None, :]
    rows_global = row_index * local_rows + jnp.arange(local_rows, dtype=jnp.int32)
    offset = cols_global - row_index * local_rows
    inside = jnp.logical_and(offset >= 0, offset < local_rows)
    block_ids = jnp.broadcast_to(
        jnp.arange(col_blocks, dtype=jnp.int32)[:, None], (col_blocks, panel_width)
    )
    lane_ids = jnp.broadcast_to(
        jnp.arange(panel_width, dtype=jnp.int32)[None, :], (col_blocks, panel_width)
    )
    front_local = front_local.at[jnp.clip(offset, 0, local_rows - 1), block_ids, lane_ids].add(
        jnp.where(inside, front_diagonal, jnp.zeros_like(front_diagonal))
    )
    for section in range(2):
        lower_panel, panel_rows = factor_panel(
            front_local, section, rows_global, cols_global, row_index, col_index
        )
        front_local = advance(front_local, lower_panel, panel_rows, section, cols_global)
    return front_local


def solution(mesh):
    in_specs = (
        P(("row", "col"), None, None),
        P(("row", "col")),
        P(("row", "col"), None),
        P(("row", "col")),
        P(None, "col"),
    )
    out_specs = P("row", None, "col")
    return jax.shard_map(
        on_device, mesh=mesh, in_specs=in_specs, out_specs=out_specs, check_vma=False
    )
```

profile of v0, /device:TPU:1, one launch (start us, length us, event | category | flops | bytes accessed | tf_op | source)
XLA Modules:
  0.0 1524.7 jit_solution(12757295335663215623)
XLA Ops:
  10.7 11.5 all-to-all-start
  23.1 11.6 broadcast_multiply_fusion
  34.7 11.3 broadcast_in_dim.129
  46.0 27.4 %scatter_fusion = f32[257,256,128]{2,1,0:T(8,128)} fusion(f32[257,256,128]{2,1,0:T(8,128)} %broadcast_in_dim.129, s32[112]{0:T(128)S(1)} %compare_select_fusion.4, f32[112,256,128]{2,1,0:T(8,128)} %broadcast_multiply_fusion), kind=kCustom, calls=%fused_computation.5 | custom fusion | bytes 44040640 | tf_op jit(solution)/shard_map/scatter | solution.py:93
  73.4 22.8 %slice.95 = f32[256,256,128]{2,1,0:T(8,128)} slice(f32[257,256,128]{2,1,0:T(8,128)} %scatter_fusion), slice={[0:256], [0:256], [0:128]} | slice | bytes 67108864 | tf_op jit(solution)/shard_map/slice | solution.py:91
  96.2 10.5 all-to-all-start.1
  110.4 518.6 %all-to-all-done.1 = f32[128,2,256,128]{3,2,1,0:T(8,128)} async-done(((f32[128,2,256,128]{3,2,1,0:T(8,128)}), f32[128,2,256,128]{3,2,1,0:T(8,128)}, u32[]{:S(2)}, u32[]{:S(2)}) %all-to-all-start.1) | async-done | bytes 33554464 | tf_op jit(solution)/shard_map/all_to_all | solution.py:99
  632.3 72.1 %scatter_fusion.1 = f32[49,256,128]{2,1,0:T(8,128)} fusion(f32[49,256,128]{2,1,0:T(8,128)} %broadcast_in_dim.123, s32[256]{0:T(256)S(1)} %bitcast.140, f32[256,256,128]{2,1,0:T(8,128)} %bitcast.4), kind=kCustom, calls=%fused_computation.6 | custom fusion | flops 8388608 | bytes 100664320 | tf_op jit(solution)/shard_map/scatter-add | solution.py:113
  704.4 6.2 slice.96
  710.6 10.3 copy.32
  721.0 9.0 reshape.313
  729.9 74.1 %scatter_fusion.2 = f32[3072,2,256]{2,0,1:T(8,128)} fusion(f32[3072,2,256]{2,0,1:T(8,128)} %reshape.313, s32[512]{0:T(512)S(1)} %bitcast.132, f32[512]{0:T(512)S(1)} %bitcast.138), kind=kCustom, calls=%fused_computation.7 | custom fusion | flops 512 | bytes 12288 | tf_op jit(solution)/shard_map/scatter-add | solution.py:130
  805.7 3.8 fusion.1
  809.8 167.3 %all-reduce.8.cloned.1.call-done = f32[256,256]{1,0:T(8,128)} async-done(((f32[256,256]{1,0:T(8,128)}), f32[256,256]{1,0:T(8,128)}) %all-reduce.8.cloned.1.call-update) | async-done | bytes 262160 | tf_op jit(solution)/shard_map/psum | solution.py:12
  979.4 11.7 cholesky.130
  991.1 9.8 custom-call.15
  1001.4 11.7 cholesky.147
  1015.2 4.2 while.4
  1020.0 19.7 %custom-call.16 = f32[2,128,128]{1,2,0:T(8,128)S(1)} custom-call(f32[2,128,128]{2,1,0:T(8,128)S(1)} %get-tuple-element.21), custom_call_target="InvertDiagBlocksLowerTriangular" | custom-call | tf_op jit(solution)/shard_map/jit(_solve_triangular)/triangular_solve | solution.py:31
  1039.7 12.3 gather_fusion
  1070.6 81.1 %all-reduce.12.cloned.1.call-done = f32[2,256,256]{2,1,0:T(8,128)} async-done(((f32[2,256,256]{2,1,0:T(8,128)}), f32[2,256,256]{2,1,0:T(8,128)}) %all-reduce.12.cloned.1.call-update) | async-done | bytes 524304 | tf_op jit(solution)/shard_map/psum | solution.py:45
  1151.8 13.4 select_select_fusion.1
  1172.8 138.3 %all-reduce.14.cloned.1.call-done = f32[256,256]{1,0:T(8,128)} async-done(((f32[256,256]{1,0:T(8,128)}), f32[256,256]{1,0:T(8,128)}) %all-reduce.14.cloned.1.call-update) | async-done | bytes 262160 | tf_op jit(solution)/shard_map/psum | solution.py:12
  1313.5 11.7 cholesky.164
  1325.3 9.8 custom-call.17
  1335.6 11.7 cholesky.181
  1350.1 4.2 while.5
  1354.3 19.7 %custom-call.18 = f32[2,128,128]{1,2,0:T(8,128)S(1)} custom-call(f32[2,128,128]{2,1,0:T(8,128)S(1)} %get-tuple-element.22), custom_call_target="InvertDiagBlocksLowerTriangular" | custom-call | tf_op jit(solution)/shard_map/jit(_solve_triangular)/triangular_solve | solution.py:31
  1374.0 12.3 gather_fusion.2
  1404.9 81.2 %all-reduce.18.cloned.1.call-done = f32[2,256,256]{2,1,0:T(8,128)} async-done(((f32[2,256,256]{2,1,0:T(8,128)}), f32[2,256,256]{2,1,0:T(8,128)}) %all-reduce.18.cloned.1.call-update) | async-done | bytes 524304 | tf_op jit(solution)/shard_map/psum | solution.py:45
  1486.1 13.7 select_select_fusion
  1499.8 17.8 %copy.46 = f32[3072,2,256]{2,1,0:T(2,128)} copy(f32[3072,2,256]{2,0,1:T(8,128)S(1)} %select_select_fusion) | data formatting | bytes 12582912 | tf_op jit(solution)/shard_map/jit(_where)/select_n | solution.py:57
  (137 shorter events, 74.1 us)
Async XLA Ops:
  10.7 85.5 %all-to-all-start = ((s32[128,1,2]{2,1,0:T(1,128)}), s32[128,1,2]{2,1,0:T(1,128)S(1)}, u32[]{:S(2)}, u32[]{:S(2)}) async-start(s32[128,1,2]{2,1,0:T(1,128)} %bitcast.1), calls=%async_computation | async-start | bytes 131072 | tf_op jit(solution)/shard_map/all_to_all | solution.py:106
  96.2 11.2 copy-start.12
  96.2 532.7 %all-to-all-start.1 = ((f32[128,2,256,128]{3,2,1,0:T(8,128)}), f32[128,2,256,128]{3,2,1,0:T(8,128)}, u32[]{:S(2)}, u32[]{:S(2)}) async-start(f32[128,2,256,128]{3,2,1,0:T(8,128)} %bitcast.131), calls=%async_computation.1 | async-start | bytes 67108864 | tf_op jit(solution)/shard_map/all_to_all | solution.py:99
  106.8 870.3 %all-reduce.8.cloned.1.call-start = ((), (), s32[]{:S(2)}) async-start(), calls=%async_computation.2 | async-start | bytes 524288 | tf_op jit(solution)/shard_map/psum | solution.py:12
  108.1 958.1 %copy-start.5 = (s32[1024]{0:T(1024)}, s32[1024]{0:T(1024)S(1)}, u32[]{:S(2)}) copy-start(s32[1024]{0:T(1024)S(1)} %pad_clamp_fusion) | copy-start | bytes 12292
  108.8 959.7 %copy-start.3 = (f32[2,256]{1,0:T(2,128)}, f32[2,256]{1,0:T(2,128)S(1)}, u32[]{:S(2)}) copy-start(f32[2,256]{1,0:T(2,128)S(1)} %get-tuple-element.61) | copy-start | bytes 6148
  805.7 248.7 %all-reduce.10.cloned.1.call-start = ((), (), s32[]{:S(2)}) async-start(), calls=%async_computation.3 | async-start | bytes 6291456 | tf_op jit(solution)/shard_map/psum | solution.py:12
  809.6 342.2 %all-reduce.12.cloned.1.call-start = ((), (), s32[]{:S(2)}) async-start(), calls=%async_computation.4 | async-start | bytes 1048576 | tf_op jit(solution)/shard_map/psum | solution.py:45
  1019.4 0.6 copy-start.13
  1054.4 3.1 copy-start.2
  1066.3 85.5 %copy-start.10 = (pred[2,256]{1,0:T(4,128)(4,1)S(1)}, pred[2,256]{1,0:T(4,128)(4,1)}, u32[]{:S(2)}) copy-start(pred[2,256]{1,0:T(4,128)(4,1)} %get-tuple-element.63) | copy-start | bytes 1540
  1066.3 85.5 %copy-start.11 = (pred[2,256]{1,0:T(4,128)(4,1)S(1)}, pred[2,256]{1,0:T(4,128)(4,1)}, u32[]{:S(2)}) copy-start(pred[2,256]{1,0:T(4,128)(4,1)} %get-tuple-element.64) | copy-start | bytes 1540
  1070.5 240.6 %all-reduce.14.cloned.1.call-start = ((), (), s32[]{:S(2)}) async-start(), calls=%async_computation.5 | async-start | bytes 524288 | tf_op jit(solution)/shard_map/psum | solution.py:12
  1165.2 2.7 copy-start
  1168.7 220.1 %all-reduce.16.cloned.1.call-start = ((), (), s32[]{:S(2)}) async-start(), calls=%async_computation.6 | async-start | bytes 6291456 | tf_op jit(solution)/shard_map/psum | solution.py:12
  1172.5 177.5 %copy-start.14 = (s32[2,2]{1,0:T(2,128)S(1)}, s32[2,2]{1,0:T(2,128)}, u32[]{:S(2)}) copy-start(s32[2,2]{1,0:T(2,128)} %copy-done.13) | copy-start | bytes 52
  1172.6 313.6 %all-reduce.18.cloned.1.call-start = ((), (), s32[]{:S(2)}) async-start(), calls=%async_computation.7 | async-start | bytes 1048576 | tf_op jit(solution)/shard_map/psum | solution.py:45
  1388.8 3.1 copy-start.1
  1391.8 4.2 copy-start.7
  1398.2 2.4 copy-start.6
  1400.6 2.3 copy-start.4
  1400.6 85.5 %copy-start.8 = (pred[2,256]{1,0:T(4,128)(4,1)S(1)}, pred[2,256]{1,0:T(4,128)(4,1)}, u32[]{:S(2)}) copy-start(pred[2,256]{1,0:T(4,128)(4,1)} %get-tuple-element.60) | copy-start | bytes 1540
  1400.6 85.5 %copy-start.9 = (pred[2,256]{1,0:T(4,128)(4,1)S(1)}, pred[2,256]{1,0:T(4,128)(4,1)}, u32[]{:S(2)}) copy-start(pred[2,256]{1,0:T(4,128)(4,1)} %get-tuple-element.62) | copy-start | bytes 1540
Sparse Core Ops, SparseCore 0:
  805.8 171.2 all-reduce.7
  979.5 65.1 all-reduce.9
  1070.7 81.0 all-reduce.11
  1168.8 142.2 all-reduce.13
  1313.5 65.2 all-reduce.15
  1405.0 81.0 all-reduce.17
where the time goes:
time: 1530 us; the launch traced here: 1520 us
  waiting for transfers between devices  987 us (65%)
  other arithmetic  291 us (19%)
  local copies, waits for them, and re-layouts  163 us (11%)
  matrix products  42.6 us (3%)
  starting transfers between devices  23.2 us (2%)
  between operations  17.5 us (1%)
    all_to_all x1, waiting for transfers between devices, on_device(): lax.all_to_all(outgoing.reshape(devices, CAP, tile_rows, tile_cols), ('ro...  519 us
    psum x4, waiting for transfers between devices, from_root(): return lax.psum(jnp.where(mine, x, jnp.zeros_like(x)), axis)  306 us
    psum x2, waiting for transfers between devices, factor_panel(): panel_rows = lax.psum(picked, 'row')  162 us
    scatter-add x1, other arithmetic, on_device(): front_local.at[jnp.clip(offset, 0, local_rows - 1), block_ids, lane_ids]  74.1 us
    scatter-add x1, other arithmetic, on_device(): jax.ops.segment_sum(arrived.reshape(-1, tile_rows, tile_cols), flat_targe...  72.1 us
    another operation x13, other arithmetic, factor_panel(): factor = jnp.linalg.cholesky(0.5 * (pivot + pivot.T))  68.7 us
    another operation x5, other arithmetic, factor_panel(): jax.scipy.linalg.solve_triangular(factor, panel_raw.T, lower=True)  39.4 us
  transfers between devices with their start and end apart: 8, of which 5 were waited for; matrix products, arithmetic and copies ran while one was open for 15% of the time, Pallas kernels for 0%

commit v1 on v0

v1 whole, which is shorter than its diff:
```python
import jax
import jax.numpy as jnp
from jax import lax
from jax.experimental import pallas as pl
from jax.experimental.pallas import tpu as pltpu
from jax.sharding import PartitionSpec as P

NF = 49152
EARLY = 8
GROUP = 8
CHUNKS = (56, 48)
BULK = 2**31
HIGHEST = lax.Precision.HIGHEST
VMEM_BYTES = 56 * 1024 * 1024


def pack_tiles(order, child_tiles, mask_columns, first, count, meta=None):
    tile_rows, tile_cols = child_tiles.shape[1:]
    stripes = tile_rows // 2
    base = first // GROUP
    extra = 0 if meta is None else meta.shape[0]
    width = 2 * GROUP + extra

    def body(order_ref, *refs):
        tiles, mask_ref = refs[:GROUP], refs[GROUP]
        out_ref, rows_ref = refs[-2], refs[-1]
        for i in range(GROUP):
            for s in range(2):
                rows = tiles[i][0, s * stripes : (s + 1) * stripes, :]
                column = mask_ref[0, s * stripes : (s + 1) * stripes, i : i + 1]
                rows_ref[pl.ds(2 * i + s, stripes, stride=2 * GROUP), :] = rows * column
        out_ref[:, : 2 * GROUP, :] = rows_ref[...].reshape(stripes, 2 * GROUP, tile_cols)
        if extra:
            meta_ref = refs[GROUP + 1]
            out_ref[:, 2 * GROUP :, :] = jnp.broadcast_to(
                meta_ref[...][None], (stripes, extra, tile_cols)
            )

    def tile_spec(i):
        return pl.BlockSpec(
            (1, tile_rows, tile_cols), lambda g, order_ref: (order_ref[first + g * GROUP + i], 0, 0)
        )

    in_specs = [tile_spec(i) for i in range(GROUP)]
    in_specs.append(pl.BlockSpec((1, tile_rows, GROUP), lambda g, order_ref: (base + g, 0, 0)))
    operands = [child_tiles] * GROUP + [mask_columns]
    if extra:
        in_specs.append(pl.BlockSpec((extra, tile_cols), lambda g, order_ref: (0, 0)))
        operands.append(meta)
    steps = count // GROUP
    return pl.pallas_call(
        body,
        grid_spec=pltpu.PrefetchScalarGridSpec(
            num_scalar_prefetch=1,
            grid=(steps,),
            in_specs=in_specs,
            out_specs=pl.BlockSpec((stripes, width, tile_cols), lambda g, order_ref: (0, g, 0)),
            scratch_shapes=[pltpu.VMEM((stripes * 2 * GROUP, tile_cols), jnp.float32)],
        ),
        out_shape=jax.ShapeDtypeStruct((stripes, steps * width, tile_cols), jnp.float32),
        compiler_params=pltpu.CompilerParams(vmem_limit_bytes=VMEM_BYTES),
        name="pack_tiles",
    )(order, *operands)


def add_pieces(targets, pieces, early, sums, first, weight):
    sources, count, two, lanes = pieces.shape
    n_sums = 6144
    per_step = 8
    fresh = sums is None

    def body(target_ref, pieces_ref, *refs):
        sums_ref = refs[-1]
        step = pl.program_id(0)

        @pl.when(step == 0)
        def _():
            sums_ref[...] = jnp.zeros_like(sums_ref) if fresh else refs[0][...]

        for n in range(per_step):
            source = step * per_step + n
            if fresh:
                for i in range(EARLY):
                    d = target_ref[source, i]
                    sums_ref[d] = sums_ref[d] + refs[0][n, i]
            for at in range(0, count, GROUP):
                ds = [target_ref[source, first + at + i] for i in range(GROUP)]
                news = [sums_ref[ds[i]] + pieces_ref[n, at + i] for i in range(GROUP)]
                for i in range(GROUP):
                    sums_ref[ds[i]] = news[i]

    def streamed(x):
        return pl.BlockSpec((per_step,) + x.shape[1:], lambda g, target_ref: (g, 0, 0, 0))

    whole = pl.BlockSpec(
        (n_sums, two, lanes), lambda g, target_ref: (0, 0, 0), pipeline_mode=pl.Buffered(1)
    )
    return pl.pallas_call(
        body,
        grid_spec=pltpu.PrefetchScalarGridSpec(
            num_scalar_prefetch=1,
            grid=(sources // per_step,),
            in_specs=[streamed(pieces), streamed(early) if fresh else whole],
            out_specs=whole,
        ),
        out_shape=jax.ShapeDtypeStruct((n_sums, two, lanes), jnp.float32),
        compiler_params=pltpu.CompilerParams(vmem_limit_bytes=VMEM_BYTES),
        cost_estimate=pl.CostEstimate(flops=weight, transcendentals=0, bytes_accessed=weight),
        name="add_pieces",
    )(targets, pieces, early if fresh else sums)


def add_top(spots, pieces, n_sums):
    sources, pitch, two, lanes = pieces.shape
    slots = spots.shape[1]

    def body(spot_ref, pieces_ref, out_ref, *parts):
        for part in parts:
            part[...] = jnp.zeros_like(part)

        def one(source, _):
            for i in range(slots):
                d = spot_ref[source, i]
                parts[i][d] = parts[i][d] + pieces_ref[source, i]
            return 0

        lax.fori_loop(0, sources, one, 0, unroll=4)
        total = parts[0][:n_sums]
        for part in parts[1:]:
            total = total + part[:n_sums]
        out_ref[...] = total

    return pl.pallas_call(
        body,
        grid_spec=pltpu.PrefetchScalarGridSpec(
            num_scalar_prefetch=1,
            grid=(1,),
            in_specs=[pl.BlockSpec(pieces.shape, lambda g, spot_ref: (0, 0, 0, 0))],
            out_specs=pl.BlockSpec((n_sums, two, lanes), lambda g, spot_ref: (0, 0, 0)),
            scratch_shapes=[pltpu.VMEM((n_sums + 8, two, lanes), jnp.float32)] * slots,
        ),
        out_shape=jax.ShapeDtypeStruct((n_sums, two, lanes), jnp.float32),
        compiler_params=pltpu.CompilerParams(vmem_limit_bytes=VMEM_BYTES),
        name="add_top",
    )(spots, pieces)


def factor_corner(corner, diagonal):
    size = corner.shape[2]
    n = 4

    def dot(a, b, transposed):
        dims = (((1,), (1 if transposed else 0,)), ((), ()))
        return lax.dot_general(a, b, dims, precision=HIGHEST, preferred_element_type=jnp.float32)

    def eliminate(block):
        groups = [block[8 * g : 8 * g + 8, :] for g in range(size // 8)]
        lane = lax.broadcasted_iota(jnp.int32, (8, size), 1)
        sub = lax.broadcasted_iota(jnp.int32, (8, size), 0)
        for p in range(size // 8):
            j0 = 8 * p
            rows = [jnp.broadcast_to(groups[p][r : r + 1, :], (8, size)) for r in range(8)]
            entry = [
                [
                    jnp.broadcast_to(rows[r][:, j0 + c : j0 + c + 1], (8, size)) if c >= r else None
                    for c in range(8)
                ]
                for r in range(8)
            ]
            ratio = [[None] * 8 for _ in range(8)]
            scaled = []
            done = groups[p]
            for r in range(8):
                row = jnp.where(jnp.logical_and(lane >= j0, lane < j0 + r), 0.0, rows[r])
                for q in range(r):
                    settled = jnp.logical_and(lane > j0 + q, lane < j0 + r)
                    row = row - ratio[r][q] * jnp.where(settled, 0.0, rows[q])
                done = jnp.where(sub == r, row, done)
                rows[r] = jnp.where(lane == j0 + r, 1.0, row)
                inverse = 1.0 / entry[r][r]
                settled = jnp.logical_and(lane > j0 + r, lane < j0 + 8)
                scaled.append(jnp.where(settled, 0.0, rows[r]) * inverse)
                for c in range(r + 1, 8):
                    ratio[c][r] = entry[r][c] * inverse
                for c in range(r + 1, 8):
                    for d in range(c, 8):
                        entry[c][d] = entry[c][d] - ratio[c][r] * entry[r][d]
            groups[p] = done
            inside = jnp.logical_and(lane >= j0, lane < j0 + 8)
            for g in range(p + 1, size // 8):
                columns = []
                result = jnp.where(inside, 0.0, groups[g])
                for c in range(8):
                    column = jnp.broadcast_to(groups[g][:, j0 + c : j0 + c + 1], (8, size))
                    for q in range(c):
                        column = column - ratio[c][q] * columns[q]
                    columns.append(column)
                    result = result - column * scaled[c]
                groups[g] = result
        return jnp.concatenate(groups, axis=0)

    def body(corner_ref, diag_ref, lower_ref, inverse_ref, flat_ref, a_ref, l_ref, i_ref):
        row = lax.broadcasted_iota(jnp.int32, (size, size), 0)
        col = lax.broadcasted_iota(jnp.int32, (size, size), 1)
        flat_ref[...] = corner_ref[...].reshape(size * 16, size)

        def raw(q, t):
            block = flat_ref[pl.ds(t * 4 + q, size, stride=16), :]
            if q == t:
                block = block + jnp.where(row == col, diag_ref[t : t + 1, :], 0.0)
            return block

        for q in range(n):
            for t in range(q + 1):
                block = raw(q, t)
                if q // 2 == t // 2:
                    block = 0.5 * (block + raw(t, q).T)
                a_ref[q * n + t] = block

        def step(k, _):
            done = eliminate(a_ref[k * n + k])
            pivots = jnp.sum(jnp.where(row == col, done, 0.0), axis=1, keepdims=True)
            root = jnp.sqrt(pivots)
            upper = jnp.where(col >= row, done, 0.0) / root
            inv = jnp.where(col < row, done, jnp.where(col == row, 1.0, 0.0)) / root
            l_ref[k * n + k] = upper.T
            i_ref[k * n + k] = inv
            for i in range(1, n):

                @pl.when(i > k)
                def _():
                    l_ref[i * n + k] = dot(a_ref[i * n + k], inv, True)

            for i in range(1, n):
                for j in range(1, i + 1):

                    @pl.when(j > k)
                    def _():
                        a_ref[i * n + j] = a_ref[i * n + j] - dot(
                            l_ref[i * n + k], l_ref[j * n + k], True
                        )

            return 0

        lax.fori_loop(0, n, step, 0)
        for i in range(n):
            for j in range(i):
                total = dot(l_ref[i * n + j], i_ref[j * n + j], False)
                for k in range(j + 1, i):
                    total = total + dot(l_ref[i * n + k], i_ref[k * n + j], False)
                i_ref[i * n + j] = -dot(i_ref[i * n + i], total, False)
        zero = jnp.zeros((size, size), jnp.float32)
        for i in range(n):
            for j in range(n):
                rows, cols = slice(i * size, (i + 1) * size), slice(j * size, (j + 1) * size)
                lower_ref[rows, cols] = l_ref[i * n + j] if j <= i else zero
                inverse_ref[rows, cols] = i_ref[i * n + j] if j <= i else zero

    shape = jax.ShapeDtypeStruct((n * size, n * size), jnp.float32)
    blocks = pltpu.VMEM((n * n, size, size), jnp.float32)
    return pl.pallas_call(
        body,
        out_shape=(shape, shape),
        scratch_shapes=[pltpu.VMEM((size * 16, size), jnp.float32), blocks, blocks, blocks],
        compiler_params=pltpu.CompilerParams(vmem_limit_bytes=VMEM_BYTES),
        name="factor_corner",
    )(corner, diagonal)


def update_rows(sums, top, inverse, own_rows, diagonal):
    blocks, n_col, halves, n_rows, lanes = sums.shape
    stripes, top_cols, _, _ = top.shape
    near = top_cols * lanes
    n_row = stripes // n_col
    share = n_rows // 2 // n_row
    pair = 8 // (blocks * halves)

    def dot(a, b, transposed):
        dims = (((1,), (1 if transposed else 0,)), ((), ()))
        return lax.dot_general(a, b, dims, precision=HIGHEST, preferred_element_type=jnp.float32)

    def body(
        sums_ref,
        panel_in_ref,
        top_ref,
        inverse_ref,
        own_ref,
        diag_ref,
        out_ref,
        panel_ref,
        factor_ref,
        flat_ref,
        result_ref,
        mixed_ref,
    ):
        g = pl.program_id(0)
        n_diag = diag_ref.shape[0]
        row = lax.broadcasted_iota(jnp.int32, (n_diag, lanes), 0)

        def with_diagonal(x, t):
            head = x[:n_diag] + jnp.where(row == t, diag_ref[...], 0.0)
            return jnp.concatenate([head, x[n_diag:]], axis=0)

        @pl.when(g == 0)
        def _():
            x = jnp.concatenate(
                [with_diagonal(panel_in_ref[0, t // 2, t % 2], t) for t in range(top_cols)], axis=1
            )
            panel = dot(x, inverse_ref[...], True)
            at = lax.broadcasted_iota(jnp.int32, (8, near), 0)
            head = jnp.where(at < 4, own_ref[...], panel[:8])
            panel = jnp.concatenate([head, panel[8:]], axis=0)
            panel_ref[...] = panel
            factor_ref[...] = dot(panel, inverse_ref[...], False)

        flat_ref[...] = top_ref[...].reshape(stripes * top_cols * 8, lanes)
        for i in range(pair):
            c = g * pair + i
            for cb in range(blocks):
                weights = jnp.concatenate(
                    [
                        jnp.concatenate(
                            [
                                flat_ref[
                                    pl.ds(
                                        k * 8 + (i * blocks + cb) * halves + h,
                                        stripes,
                                        stride=top_cols * 8,
                                    ),
                                    :,
                                ]
                                for k in range(top_cols)
                            ],
                            axis=1,
                        )
                        for h in range(halves)
                    ],
                    axis=0,
                )
                product = dot(factor_ref[...], weights, True)
                for h in range(halves):
                    t = (cb * n_col + c) * halves + h
                    result = with_diagonal(sums_ref[cb, i, h], t)
                    result = result - product[:, h * lanes : (h + 1) * lanes]
                    if cb == 0:
                        at = (i * halves + h) * lanes
                        result = jnp.where(g == 0, panel_ref[:, at : at + lanes], result)
                    result_ref[...] = result
                    for s in range(2):
                        mixed_ref[pl.ds(s * 4 + h * 2 + cb, n_rows // 2, stride=8), :] = result_ref[
                            pl.ds(s, n_rows // 2, stride=2), :
                        ]
            out_ref[:, i] = mixed_ref[...].reshape(n_row, share * 8, lanes)

    def fixed(*shape):
        return pl.BlockSpec(shape, lambda g: (0,) * len(shape))

    return pl.pallas_call(
        body,
        grid=(n_col // pair,),
        in_specs=[
            pl.BlockSpec((blocks, pair, halves, n_rows, lanes), lambda g: (0, g, 0, 0, 0)),
            pl.BlockSpec((1, 2, halves, n_rows, lanes), lambda g: (0, 0, 0, 0, 0)),
            pl.BlockSpec((stripes, top_cols, 8, lanes), lambda g: (0, 0, g, 0)),
            fixed(near, near),
            fixed(8, near),
            fixed(*diagonal.shape),
        ],
        out_specs=pl.BlockSpec((n_row, pair, share * 8, lanes), lambda g: (0, g, 0, 0)),
        out_shape=jax.ShapeDtypeStruct((n_row, n_col, share * 8, lanes), jnp.float32),
        scratch_shapes=[
            pltpu.VMEM((n_rows, near), jnp.float32),
            pltpu.VMEM((n_rows, near), jnp.float32),
            pltpu.VMEM((stripes * top_cols * 8, lanes), jnp.float32),
            pltpu.VMEM((n_rows, lanes), jnp.float32),
            pltpu.VMEM((n_rows * 4, lanes), jnp.float32),
        ],
        compiler_params=pltpu.CompilerParams(vmem_limit_bytes=VMEM_BYTES),
        name="update_rows",
    )(sums, sums, top, inverse, own_rows, diagonal)


def place_rows(received):
    stripes, width, lanes = received.shape
    row_tiles = width // 8

    def body(in_ref, out_ref, flat_ref):
        flat_ref[...] = in_ref[...].reshape(stripes * 8, lanes)
        for s in range(2):
            for k in range(4):
                out_ref[pl.ds(s * stripes * 4 + k, stripes, stride=4), :] = flat_ref[
                    pl.ds(s * 4 + k, stripes, stride=8), :
                ]

    return pl.pallas_call(
        body,
        grid=(row_tiles,),
        in_specs=[pl.BlockSpec((stripes, 8, lanes), lambda g: (0, g, 0))],
        out_specs=pl.BlockSpec((stripes * 8, lanes), lambda g: (g, 0)),
        out_shape=jax.ShapeDtypeStruct((row_tiles * stripes * 8, lanes), jnp.float32),
        scratch_shapes=[pltpu.VMEM((stripes * 8, lanes), jnp.float32)],
        compiler_params=pltpu.CompilerParams(vmem_limit_bytes=VMEM_BYTES),
        name="place_rows",
    )(received)


def tile_order(tile_dest, col_tiles, top_rows, top_cols):
    total = tile_dest.shape[0]
    ids = jnp.arange(total, dtype=jnp.int32)
    same = tile_dest[:, None] == tile_dest[None, :]
    first_of = jnp.min(jnp.where(same, ids[None, :], total), axis=1)
    later = jnp.any(jnp.logical_and(same, ids[None, :] > ids[:, None]), axis=1)
    top = jnp.logical_and(tile_dest // col_tiles < top_rows, tile_dest % col_tiles < top_cols)
    rest = jnp.where(
        first_of < ids, 3 * total + first_of, jnp.where(later, total + ids, 2 * total + ids)
    )
    key = jnp.where(top, ids, rest)
    position = jnp.sum((key[None, :] < key[:, None]).astype(jnp.int32), axis=1)
    return (position[:, None] == ids[None, :]).astype(jnp.int32)


def on_device(child_tiles, tile_dest, tile_mask, tile_count, front_diagonal):
    axes = ("row", "col")
    n_row = lax.axis_size("row")
    n_col = lax.axis_size("col")
    devices = n_row * n_col
    me = lax.axis_index("row") * n_col + lax.axis_index("col")
    tile_total, tile_rows, lanes = child_tiles.shape
    col_blocks, panel = front_diagonal.shape
    halves = panel // lanes
    row_tiles = NF // tile_rows
    col_tiles = col_blocks * n_col * halves
    width = col_tiles * lanes
    top_rows = width // tile_rows
    top_cols = 2 * halves

    placed = tile_order(tile_dest, col_tiles, top_rows, top_cols)
    ids = jnp.arange(tile_total, dtype=jnp.int32)
    target = (tile_dest % col_tiles) * row_tiles + tile_dest // col_tiles
    order = jnp.sum(placed * ids[:, None], axis=0)
    target_sent = jnp.sum(placed * target[:, None], axis=0)
    live = (ids < tile_count[0]).astype(jnp.float32)
    mask_columns = lax.dot_general(
        tile_mask.astype(jnp.float32),
        placed.astype(jnp.float32) * live[:, None],
        (((0,), (0,)), ((), ())),
    )
    mask_columns = mask_columns.reshape(tile_rows, tile_total // GROUP, GROUP).transpose(1, 0, 2)
    meta = jnp.concatenate(
        [
            jnp.pad(target_sent.astype(jnp.float32), (0, lanes - tile_total))[None],
            front_diagonal.reshape(col_blocks * halves, lanes),
            jnp.zeros((8 - 1 - col_blocks * halves, lanes), jnp.float32),
        ],
        axis=0,
    )

    def exchange(x):
        return lax.all_to_all(x, axes, split_axis=0, concat_axis=0, tiled=True)

    early = exchange(pack_tiles(order, child_tiles, mask_columns, 0, EARLY, meta))
    at = EARLY
    first_pack = pack_tiles(order, child_tiles, mask_columns, at, CHUNKS[0])
    early, first_pack = lax.optimization_barrier((early, first_pack))
    received0 = exchange(first_pack)

    targets = early[:, 2 * EARLY, :].astype(jnp.int32)
    diagonal = early[:n_col, 2 * EARLY + 1 : 2 * EARLY + 1 + col_blocks * halves, :]
    diagonal = diagonal.reshape(n_col, col_blocks, panel).transpose(1, 0, 2)
    diagonal = diagonal.reshape(col_tiles, lanes)
    early = early.reshape(devices, EARLY + 4, 2, lanes)
    n_top = top_cols * top_rows
    tile, row = targets[:, :EARLY] // row_tiles, targets[:, :EARLY] % row_tiles
    spots = tile * top_rows + row % n_col * col_blocks + row // n_col
    spots = jnp.where(jnp.logical_and(tile < top_cols, row < top_rows), spots, n_top)
    view = add_top(spots, early, n_top)
    top = lax.all_gather(view.reshape(top_cols, 2 * top_rows, lanes), "col")
    top = lax.all_gather(top, "row").reshape(devices, top_cols, 2 * top_rows, lanes)

    second_pack = pack_tiles(order, child_tiles, mask_columns, at + CHUNKS[0], CHUNKS[1])
    received0, second_pack = lax.optimization_barrier((received0, second_pack))
    received1 = exchange(second_pack)
    pieces = received0.reshape(devices, CHUNKS[0], 2, lanes)
    sums = add_pieces(targets, pieces, early, None, at, BULK)
    top, sums = lax.optimization_barrier((top, sums))
    corner = top.reshape(devices, top_cols, n_col, col_blocks, 2, lanes)[:, :, :2, 0]
    lower, inverse = factor_corner(corner.reshape(devices, 4 * top_cols, lanes), diagonal[:8])
    own_rows = lax.dynamic_slice(
        lower.reshape(top_cols, devices, top_cols * lanes),
        (0, me, 0),
        (top_cols, 1, top_cols * lanes),
    )
    own_rows = jnp.pad(own_rows.reshape(top_cols, top_cols * lanes), ((0, 8 - top_cols), (0, 0)))
    received1, inverse, own_rows = lax.optimization_barrier((received1, inverse, own_rows))
    pieces = received1.reshape(devices, CHUNKS[1], 2, lanes)
    sums = add_pieces(targets, pieces, None, sums, at + CHUNKS[0], BULK)

    own = jnp.where(jnp.arange(lanes, dtype=jnp.int32)[None, :] == me, diagonal, 0.0)
    result = update_rows(
        sums.reshape(col_blocks, n_col, halves, 2 * row_tiles, lanes), top, inverse, own_rows, own
    )
    received = exchange(result.reshape(devices, -1, lanes))
    rows = place_rows(received)
    rows = rows.reshape(NF // n_row, halves, col_blocks, lanes).transpose(0, 2, 1, 3)
    return rows.reshape(NF // n_row, col_blocks, panel)


def solution(mesh):
    in_specs = (
        P(("row", "col"), None, None),
        P(("row", "col")),
        P(("row", "col"), None),
        P(("row", "col")),
        P(None, "col"),
    )
    out_specs = P("row", None, "col")
    return jax.shard_map(
        on_device, mesh=mesh, in_specs=in_specs, out_specs=out_specs, check_vma=False
    )
```

time: 1530 us -> 460 us (0.30)
  waiting for transfers between devices: 987 us -> 163 us
  other arithmetic: 291 us -> 5.39 us
  local copies, waits for them, and re-layouts: 163 us -> 8.35 us
  Pallas kernels: 0 us -> 130 us
  blocking collectives: 0 us -> 109 us
  matrix products: 42.6 us -> 1.17 us
    psum x6 -> x0, waiting for transfers between devices: 468 us -> none  [the longest x4 306 us: from_root(): return lax.psum(jnp.where(mine, x, jnp.zeros_like(x)), axis)]
    all_to_all x2 -> x3, waiting for transfers between devices: 519 us -> 101 us  [exchange(): return lax.all_to_all(x, axes, split_axis=0, concat_axis=0, tiled=True)]
    scatter-add x2 -> x0, other arithmetic: 146 us -> none  [the longest x1 74.1 us: on_device(): front_local.at[jnp.clip(offset, 0, local_rows - 1), block_ids, lane_ids]]
    pallas_call x0 -> x9, Pallas kernels: none -> 130 us  [the longest x2 42.3 us: add_pieces(): pl.pallas_call(body, grid_spec=pltpu.PrefetchScalarGridSpec(num_scalar_pr...]
    another operation x19 -> x0, other arithmetic: 108 us -> none  [the longest x13 68.7 us: factor_panel(): factor = jnp.linalg.cholesky(0.5 * (pivot + pivot.T))]
    all_to_all x0 -> x1, blocking collectives: none -> 93.4 us  [exchange(): return lax.all_to_all(x, axes, split_axis=0, concat_axis=0, tiled=True)]
    all_gather x0 -> x1, waiting for transfers between devices: none -> 62.3 us  [on_device(): lax.all_gather(top, 'row').reshape(devices, top_cols, 2 * top_rows, lanes)]
    gather x6 -> x0, local copies, waits for them, and re-layouts: 33.9 us -> none  [the longest x4 29.4 us: factor_panel(): factor_rows = factor[inner_row]]
  transfers between devices with their start and end apart: 8 -> 4, of which waited for: 5 -> 3; matrix products, arithmetic and copies ran while one was open for 15% -> 1% of each run, Pallas kernels for 0% -> 15%
where the time goes in v1:
time: 460 us; the launch traced here: 458 us
  waiting for transfers between devices  163 us (35%)
  Pallas kernels  130 us (28%)
  blocking collectives  109 us (24%)
  starting transfers between devices  26.6 us (6%)
  between operations  14.2 us (3%)
  local copies, waits for them, and re-layouts  8.35 us (2%)
  other arithmetic  5.39 us (1%)
    all_to_all x3, waiting for transfers between devices, exchange(): return lax.all_to_all(x, axes, split_axis=0, concat_axis=0, tiled=True)  101 us
    all_to_all x1, blocking collectives, exchange(): return lax.all_to_all(x, axes, split_axis=0, concat_axis=0, tiled=True)  93.4 us
    all_gather x1, waiting for transfers between devices, on_device(): lax.all_gather(top, 'row').reshape(devices, top_cols, 2 * top_rows, lanes)  62.3 us
    pallas_call x2, Pallas kernels, add_pieces(): pl.pallas_call(body, grid_spec=pltpu.PrefetchScalarGridSpec(num_scalar_pr...  42.3 us
    all_to_all x3, starting transfers between devices, exchange(): return lax.all_to_all(x, axes, split_axis=0, concat_axis=0, tiled=True)  26.6 us
    pallas_call x1, Pallas kernels, factor_corner(): pl.pallas_call(body, out_shape=(shape, shape), scratch_shapes=[pltpu.VMEM...  26 us
    pallas_call x3, Pallas kernels, pack_tiles(): pl.pallas_call(body, grid_spec=pltpu.PrefetchScalarGridSpec(num_scalar_pr...  23.9 us
    pallas_call x1, Pallas kernels, update_rows(): pl.pallas_call(body, grid=(n_col // pair,), in_specs=[pl.BlockSpec((block...  22.8 us
  transfers between devices with their start and end apart: 4, of which 3 were waited for; matrix products, arithmetic and copies ran while one was open for 1% of the time, Pallas kernels for 15%

profile of v1, /device:TPU:1, one launch (start us, length us, event | category | flops | bytes accessed | tf_op | source)
XLA Modules:
  0.0 457.8 jit_solution(8171240042696154977)
XLA Ops:
  6.5 0.9 fusion.11
  7.5 0.9 fusion.15
  9.1 0.7 and_select_fusion
  9.9 0.6 select_reduce_fusion
  10.5 0.7 reshape.63
  11.2 1.2 convolution_bitcast_fusion
  12.4 1.8 copy.23
  14.2 0.7 maximum_maximum_fusion.refs_9_
  14.9 3.8 pack_tiles.3
  18.7 11.5 %all-to-all-start = ((f32[128,24,128]{2,1,0:T(8,128)}), f32[128,24,128]{2,1,0:T(8,128)S(1)}, u32[]{:S(2)}, u32[]{:S(2)}) async-start(f32[128,24,128]{2,1,0:T(8,128)} %pack_tiles.3), calls=%async_computation | async-start | bytes 3145728 | tf_op jit(solution)/shard_map/all_to_all | solution.py:459
  30.3 10.8 %pack_tiles.4 = f32[128,112,128]{2,1,0:T(8,128)} custom-call(s32[112]{0:T(128)} %get-tuple-element.28.order_ref, f32[112,256,128]{2,1,0:T(8,128)} %refs_7_.5, f32[112,256,128]{2,1,0:T(8,128)} %refs_7_.5, f32[112,256,128]{2,1,0:T(8,128)} %refs_7_.5, f32[112,256,128]{2,1,0:T(8,128)} %refs_7_.5, f32[112,256,128]{2,1,0:T(8,128)} %refs_7_.5, ...), custom_call_target="tpu_custom_call" | custom-call | tf_op jit(solution)/shard_map/pack_tiles/pallas_call | solution.py:51
  41.0 14.1 %all-to-all-done = f32[128,24,128]{2,1,0:T(8,128)S(1)} async-done(((f32[128,24,128]{2,1,0:T(8,128)}), f32[128,24,128]{2,1,0:T(8,128)S(1)}, u32[]{:S(2)}, u32[]{:S(2)}) %all-to-all-start) | async-done | bytes 1572896 | tf_op jit(solution)/shard_map/all_to_all | solution.py:459
  55.4 0.8 fusion.4.spot_ref
  56.3 5.3 %add_top.1 = f32[64,2,128]{2,1,0:T(2,128)} custom-call(s32[128,8]{1,0:T(8,128)} %fusion.4.spot_ref, f32[128,12,2,128]{3,2,1,0:T(2,128)} %bitcast.38), custom_call_target="tpu_custom_call" | custom-call | tf_op jit(solution)/shard_map/add_top/pallas_call | solution.py:133
  61.6 15.4 %all_gather.9 = f32[8,4,32,128]{3,2,1,0:T(8,128)} all-gather(f32[1,4,32,128]{3,2,1,0:T(8,128)} %bitcast.43), channel_id=1, replica_groups=mesh['row'=16,'col'=8] {'col'}, dimensions={0}, use_global_device_ids=true | all-gather | bytes 589824 | tf_op jit(solution)/shard_map/all_gather | solution.py:477
  77.0 4.8 %all-to-all-start.1 = ((f32[128,112,128]{2,1,0:T(8,128)}), f32[128,112,128]{2,1,0:T(8,128)}, u32[]{:S(2)}, u32[]{:S(2)}) async-start(f32[128,112,128]{2,1,0:T(8,128)} %pack_tiles.4), calls=%async_computation.1 | async-start | bytes 14680064 | tf_op jit(solution)/shard_map/all_to_all | solution.py:459
  81.8 9.4 %pack_tiles.5 = f32[128,96,128]{2,1,0:T(8,128)} custom-call(s32[112]{0:T(128)} %get-tuple-element.28.order_ref, f32[112,256,128]{2,1,0:T(8,128)} %refs_7_.5, f32[112,256,128]{2,1,0:T(8,128)} %refs_7_.5, f32[112,256,128]{2,1,0:T(8,128)} %refs_7_.5, f32[112,256,128]{2,1,0:T(8,128)} %refs_7_.5, f32[112,256,128]{2,1,0:T(8,128)} %refs_7_.5, ...), custom_call_target="tpu_custom_call" | custom-call | tf_op jit(solution)/shard_map/pack_tiles/pallas_call | solution.py:51
  91.1 86.8 %all-to-all-done.1 = f32[128,112,128]{2,1,0:T(8,128)} async-done(((f32[128,112,128]{2,1,0:T(8,128)}), f32[128,112,128]{2,1,0:T(8,128)}, u32[]{:S(2)}, u32[]{:S(2)}) %all-to-all-start.1) | async-done | bytes 7340064 | tf_op jit(solution)/shard_map/all_to_all | solution.py:459
  177.9 10.3 %all-to-all-start.2 = ((f32[128,96,128]{2,1,0:T(8,128)}), f32[128,96,128]{2,1,0:T(8,128)}, u32[]{:S(2)}, u32[]{:S(2)}) async-start(f32[128,96,128]{2,1,0:T(8,128)} %pack_tiles.5), calls=%async_computation.2 | async-start | bytes 12582912 | tf_op jit(solution)/shard_map/all_to_all | solution.py:459
  188.3 0.8 slice.19
  189.1 0.6 slice.24.diag_ref
  189.7 0.6 broadcast_select_fusion.diag_ref
  190.3 22.3 %add_pieces.2.refs_0_ = f32[6144,2,128]{2,1,0:T(2,128)} custom-call(s32[128,128]{1,0:T(8,128)} %copy-done.1, f32[128,56,2,128]{3,2,1,0:T(2,128)} %bitcast.8.pieces_ref, f32[128,12,2,128]{3,2,1,0:T(2,128)} %bitcast.39), custom_call_target="tpu_custom_call" | custom-call | flops 2147483648 | bytes 2147483648 | tf_op jit(solution)/shard_map/add_pieces/pallas_call | solution.py:98
  212.5 62.3 %all-gather.3.cloned.1.call-done.top_ref = f32[128,4,32,128]{3,2,1,0:T(8,128)} async-done(((f32[8,4,32,128]{3,2,1,0:T(8,128)}), f32[128,4,32,128]{3,2,1,0:T(8,128)}) %all-gather.3.cloned.1.call-update) | async-done | bytes 8388624 | tf_op jit(solution)/shard_map/all_gather | solution.py:478
  274.8 2.6 slice.23
  277.4 26.0 %factor_corner.1 = (f32[512,512]{1,0:T(8,128)}, f32[512,512]{1,0:T(8,128)}) custom-call(f32[128,16,128]{2,1,0:T(8,128)} %bitcast.42, f32[8,128]{1,0:T(8,128)} %slice.24.diag_ref), custom_call_target="tpu_custom_call" | custom-call | tf_op jit(solution)/shard_map/factor_corner/pallas_call | solution.py:261
  303.4 0.8 constant_dynamic-slice_fusion
  304.3 0.6 pad.9.own_ref
  304.9 20.1 %add_pieces.3 = f32[6144,2,128]{2,1,0:T(2,128)} custom-call(s32[128,128]{1,0:T(8,128)} %copy-done.1, f32[128,48,2,128]{3,2,1,0:T(2,128)} %bitcast.14.pieces_ref, f32[6144,2,128]{2,1,0:T(2,128)} %add_pieces.2.refs_0_), custom_call_target="tpu_custom_call" | custom-call | flops 2147483648 | bytes 2147483648 | tf_op jit(solution)/shard_map/add_pieces/pallas_call | solution.py:98
  324.9 22.8 %update_rows.1 = f32[16,8,96,128]{3,2,1,0:T(8,128)} custom-call(f32[2,8,2,384,128]{4,3,2,1,0:T(8,128)} %bitcast.33, f32[2,8,2,384,128]{4,3,2,1,0:T(8,128)} %bitcast.34, f32[128,4,32,128]{3,2,1,0:T(8,128)} %all-gather.3.cloned.1.call-done.top_ref, f32[512,512]{1,0:T(8,128)} %get-tuple-element.25.inverse_ref, f32[8,512]{1,0:T(8,128)} %pad.9.own_ref, ...), custom_call_target="tpu_custom_call" | custom-call | tf_op jit(solution)/shard_map/update_rows/pallas_call | solution.py:358
  347.7 93.4 %all_to_all.20.in_ref = f32[128,96,128]{2,1,0:T(8,128)} all-to-all(f32[128,96,128]{2,1,0:T(8,128)} %bitcast.40), channel_id=1, replica_groups=mesh['row'=16,'col'=8] {'row','col'}, dimensions={0} | all-to-all | bytes 12582912 | tf_op jit(solution)/shard_map/all_to_all | solution.py:459
  441.1 9.8 %place_rows.1 = f32[12288,128]{1,0:T(8,128)} custom-call(f32[128,96,128]{2,1,0:T(8,128)} %all_to_all.20.in_ref), custom_call_target="tpu_custom_call" | custom-call | tf_op jit(solution)/shard_map/place_rows/pallas_call | solution.py:395
  (21 shorter events, 0.7 us)
Async XLA Ops:
  18.7 36.4 %all-to-all-start = ((f32[128,24,128]{2,1,0:T(8,128)}), f32[128,24,128]{2,1,0:T(8,128)S(1)}, u32[]{:S(2)}, u32[]{:S(2)}) async-start(f32[128,24,128]{2,1,0:T(8,128)} %pack_tiles.3), calls=%async_computation | async-start | bytes 3145728 | tf_op jit(solution)/shard_map/all_to_all | solution.py:459
  30.2 244.6 %all-gather.3.cloned.1.call-start = ((), (), s32[]{:S(2)}) async-start(), calls=%async_computation.4 | async-start | bytes 8912896 | tf_op jit(solution)/shard_map/all_gather | solution.py:478
  55.1 1.2 copy-start
  55.4 21.5 %copy-start.1 = (s32[128,128]{1,0:T(8,128)}, s32[128,128]{1,0:T(8,128)S(1)}, u32[]{:S(2)}) copy-start(s32[128,128]{1,0:T(8,128)S(1)} %fusion.5.target_ref) | copy-start | bytes 196612
  77.0 101.0 %all-to-all-start.1 = ((f32[128,112,128]{2,1,0:T(8,128)}), f32[128,112,128]{2,1,0:T(8,128)}, u32[]{:S(2)}, u32[]{:S(2)}) async-start(f32[128,112,128]{2,1,0:T(8,128)} %pack_tiles.4), calls=%async_computation.1 | async-start | bytes 14680064 | tf_op jit(solution)/shard_map/all_to_all | solution.py:459
  177.9 126.9 %all-to-all-start.2 = ((f32[128,96,128]{2,1,0:T(8,128)}), f32[128,96,128]{2,1,0:T(8,128)}, u32[]{:S(2)}, u32[]{:S(2)}) async-start(f32[128,96,128]{2,1,0:T(8,128)} %pack_tiles.5), calls=%async_computation.2 | async-start | bytes 12582912 | tf_op jit(solution)/shard_map/all_to_all | solution.py:459
Sparse Core Ops, SparseCore 0:
  77.1 197.6 all-gather.2

commit v2 on v1

--- a/solution.py
+++ b/solution.py
@@ -382,26 +382,21 @@
 
 def place_rows(received):
     stripes, width, lanes = received.shape
-    row_tiles = width // 8
-
-    def body(in_ref, out_ref, flat_ref):
-        flat_ref[...] = in_ref[...].reshape(stripes * 8, lanes)
+    units = width // 4
+
+    def body(in_ref, out_ref):
         for s in range(2):
-            for k in range(4):
-                out_ref[pl.ds(s * stripes * 4 + k, stripes, stride=4), :] = flat_ref[
-                    pl.ds(s * 4 + k, stripes, stride=8), :
-                ]
+            out_ref[s] = in_ref[:, s]
 
     return pl.pallas_call(
         body,
-        grid=(row_tiles,),
-        in_specs=[pl.BlockSpec((stripes, 8, lanes), lambda g: (0, g, 0))],
-        out_specs=pl.BlockSpec((stripes * 8, lanes), lambda g: (g, 0)),
-        out_shape=jax.ShapeDtypeStruct((row_tiles * stripes * 8, lanes), jnp.float32),
-        scratch_shapes=[pltpu.VMEM((stripes * 8, lanes), jnp.float32)],
+        grid=(units // 2,),
+        in_specs=[pl.BlockSpec((stripes, 2, 4, lanes), lambda g: (0, g, 0, 0))],
+        out_specs=pl.BlockSpec((2, stripes, 4, lanes), lambda g: (g, 0, 0, 0)),
+        out_shape=jax.ShapeDtypeStruct((units, stripes, 4, lanes), jnp.float32),
         compiler_params=pltpu.CompilerParams(vmem_limit_bytes=VMEM_BYTES),
         name="place_rows",
-    )(received)
+    )(received.reshape(stripes, units, 4, lanes))
 
 
 def tile_order(tile_dest, col_tiles, top_rows, top_cols):
@@ -474,15 +469,29 @@
     spots = tile * top_rows + row % n_col * col_blocks + row // n_col
     spots = jnp.where(jnp.logical_and(tile < top_cols, row < top_rows), spots, n_top)
     view = add_top(spots, early, n_top)
-    top = lax.all_gather(view.reshape(top_cols, 2 * top_rows, lanes), "col")
-    top = lax.all_gather(top, "row").reshape(devices, top_cols, 2 * top_rows, lanes)
+    share = lax.all_gather(view.reshape(top_cols, 2 * top_rows, lanes), "row")
 
     second_pack = pack_tiles(order, child_tiles, mask_columns, at + CHUNKS[0], CHUNKS[1])
-    received0, second_pack = lax.optimization_barrier((received0, second_pack))
+    received0, second_pack, share = lax.optimization_barrier((received0, second_pack, share))
+    chips = n_col // 2
+    my_chip, my_core = lax.axis_index("col") // 2, lax.axis_index("col") % 2
+    half_top = jnp.zeros((n_row, chips) + share.shape[1:], jnp.float32)
+    for step in range(chips):
+        moved = share
+        if step:
+            hops = [(2 * i + k, 2 * ((i + step) % chips) + k) for i in range(chips) for k in range(2)]
+            moved = lax.ppermute(share, "col", hops)
+        origin = (my_chip + chips - step) % chips
+        half_top = lax.dynamic_update_slice(half_top, moved[:, None], (0, origin, 0, 0, 0))
     received1 = exchange(second_pack)
     pieces = received0.reshape(devices, CHUNKS[0], 2, lanes)
     sums = add_pieces(targets, pieces, early, None, at, BULK)
-    top, sums = lax.optimization_barrier((top, sums))
+    half_top, sums = lax.optimization_barrier((half_top, sums))
+    other_top = lax.ppermute(half_top, "col", [(i, i + 1 - 2 * (i % 2)) for i in range(n_col)])
+    top = jnp.where(
+        my_core == jnp.arange(2).reshape(1, 1, 2, 1, 1, 1), half_top[:, :, None], other_top[:, :, None]
+    )
+    top = top.reshape(devices, top_cols, 2 * top_rows, lanes)
     corner = top.reshape(devices, top_cols, n_col, col_blocks, 2, lanes)[:, :, :2, 0]
     lower, inverse = factor_corner(corner.reshape(devices, 4 * top_cols, lanes), diagonal[:8])
     own_rows = lax.dynamic_slice(

time: 460 us -> 482 us (1.048)
  waiting for transfers between devices: 163 us -> 190 us
  blocking collectives: 109 us -> 82.1 us
  local copies, waits for them, and re-layouts: 8.35 us -> 18.2 us
  other arithmetic: 5.39 us -> 13.1 us
    ppermute x0 -> x4, waiting for transfers between devices: none -> 93.9 us  [the longest x3 89 us: on_device(): moved = lax.ppermute(share, 'col', hops)]
    all_to_all x3, waiting for transfers between devices: 101 us -> 14.1 us  [exchange(): return lax.all_to_all(x, axes, split_axis=0, concat_axis=0, tiled=True)]
    all_gather x1, waiting for transfers between devices: 62.3 us -> 82 us  [on_device(): share = lax.all_gather(view.reshape(top_cols, 2 * top_rows, lanes), 'row')]
    all_gather x1 -> x0, blocking collectives: 15.4 us -> none  [on_device(): top = lax.all_gather(view.reshape(top_cols, 2 * top_rows, lanes), 'col')]
    all_to_all x1, blocking collectives: 93.4 us -> 82.1 us  [exchange(): return lax.all_to_all(x, axes, split_axis=0, concat_axis=0, tiled=True)]
    select_n x0 -> x2, other arithmetic: none -> 7.69 us  [on_device(): jnp.where(my_core == jnp.arange(2).reshape(1, 1, 2, 1, 1, 1), half_top[:,...]
    broadcast_in_dim x0 -> x5, local copies, waits for them, and re-layouts: none -> 7.44 us  [the longest x4 6.92 us: on_device(): jnp.where(my_core == jnp.arange(2).reshape(1, 1, 2, 1, 1, 1), half_top[:,...]
    dynamic_update_slice x0 -> x5, local copies, waits for them, and re-layouts: none -> 5.09 us  [on_device(): lax.dynamic_update_slice(half_top, moved[:, None], (0, origin, 0, 0, 0))]
  transfers between devices with their start and end apart: 4 -> 8, of which waited for: 3 -> 6; matrix products, arithmetic and copies ran while one was open for 1% -> 5% of each run, Pallas kernels for 15% -> 15%
where the time goes in v2:
time: 482 us; the launch traced here: 480 us
  waiting for transfers between devices  190 us (39%)
  Pallas kernels  130 us (27%)
  blocking collectives  82.1 us (17%)
  starting transfers between devices  30.8 us (6%)
  local copies, waits for them, and re-layouts  18.2 us (4%)
  between operations  14.3 us (3%)
  other arithmetic  13.1 us (3%)
    ppermute x3, waiting for transfers between devices, on_device(): moved = lax.ppermute(share, 'col', hops)  89 us
    all_to_all x1, blocking collectives, exchange(): return lax.all_to_all(x, axes, split_axis=0, concat_axis=0, tiled=True)  82.1 us
    all_gather x1, waiting for transfers between devices, on_device(): share = lax.all_gather(view.reshape(top_cols, 2 * top_rows, lanes), 'row')  82 us
    pallas_call x2, Pallas kernels, add_pieces(): pl.pallas_call(body, grid_spec=pltpu.PrefetchScalarGridSpec(num_scalar_pr...  42.2 us
    pallas_call x1, Pallas kernels, factor_corner(): pl.pallas_call(body, out_shape=(shape, shape), scratch_shapes=[pltpu.VMEM...  26 us
    all_to_all x3, starting transfers between devices, exchange(): return lax.all_to_all(x, axes, split_axis=0, concat_axis=0, tiled=True)  25.9 us
    pallas_call x3, Pallas kernels, pack_tiles(): pl.pallas_call(body, grid_spec=pltpu.PrefetchScalarGridSpec(num_scalar_pr...  23.8 us
    pallas_call x1, Pallas kernels, update_rows(): pl.pallas_call(body, grid=(n_col // pair,), in_specs=[pl.BlockSpec((block...  22.8 us
  transfers between devices with their start and end apart: 8, of which 6 were waited for; matrix products, arithmetic and copies ran while one was open for 5% of the time, Pallas kernels for 15%

profile of v2, /device:TPU:1, one launch (start us, length us, event | category | flops | bytes accessed | tf_op | source)
XLA Modules:
  0.0 479.5 jit_solution(10277551165069930127)
XLA Ops:
  6.5 0.9 fusion.11
  7.5 0.9 fusion.15
  10.6 1.2 convolution_bitcast_fusion
  11.8 1.8 copy.38
  15.0 3.8 pack_tiles.3
  18.8 11.5 %all-to-all-start = ((f32[128,24,128]{2,1,0:T(8,128)}), f32[128,24,128]{2,1,0:T(8,128)S(1)}, u32[]{:S(2)}, u32[]{:S(2)}) async-start(f32[128,24,128]{2,1,0:T(8,128)} %pack_tiles.3), calls=%async_computation | async-start | bytes 3145728 | tf_op jit(solution)/shard_map/all_to_all | solution.py:454
  30.3 10.8 %pack_tiles.4 = f32[128,112,128]{2,1,0:T(8,128)} custom-call(s32[112]{0:T(128)} %get-tuple-element.30.order_ref, f32[112,256,128]{2,1,0:T(8,128)} %refs_7_.5, f32[112,256,128]{2,1,0:T(8,128)} %refs_7_.5, f32[112,256,128]{2,1,0:T(8,128)} %refs_7_.5, f32[112,256,128]{2,1,0:T(8,128)} %refs_7_.5, f32[112,256,128]{2,1,0:T(8,128)} %refs_7_.5, ...), custom_call_target="tpu_custom_call" | custom-call | tf_op jit(solution)/shard_map/pack_tiles/pallas_call | solution.py:51
  41.1 14.1 %all-to-all-done = f32[128,24,128]{2,1,0:T(8,128)S(1)} async-done(((f32[128,24,128]{2,1,0:T(8,128)}), f32[128,24,128]{2,1,0:T(8,128)S(1)}, u32[]{:S(2)}, u32[]{:S(2)}) %all-to-all-start) | async-done | bytes 1572896 | tf_op jit(solution)/shard_map/all_to_all | solution.py:454
  55.2 5.7 %all-to-all-start.1 = ((f32[128,112,128]{2,1,0:T(8,128)}), f32[128,112,128]{2,1,0:T(8,128)}, u32[]{:S(2)}, u32[]{:S(2)}) async-start(f32[128,112,128]{2,1,0:T(8,128)} %pack_tiles.4), calls=%async_computation.1 | async-start | bytes 14680064 | tf_op jit(solution)/shard_map/all_to_all | solution.py:454
  62.1 5.3 %add_top.1 = f32[64,2,128]{2,1,0:T(2,128)} custom-call(s32[128,8]{1,0:T(8,128)} %fusion.4.spot_ref, f32[128,12,2,128]{3,2,1,0:T(2,128)} %bitcast.52), custom_call_target="tpu_custom_call" | custom-call | tf_op jit(solution)/shard_map/add_top/pallas_call | solution.py:133
  67.4 9.3 %pack_tiles.5 = f32[128,96,128]{2,1,0:T(8,128)} custom-call(s32[112]{0:T(128)} %get-tuple-element.30.order_ref, f32[112,256,128]{2,1,0:T(8,128)} %refs_7_.5, f32[112,256,128]{2,1,0:T(8,128)} %refs_7_.5, f32[112,256,128]{2,1,0:T(8,128)} %refs_7_.5, f32[112,256,128]{2,1,0:T(8,128)} %refs_7_.5, f32[112,256,128]{2,1,0:T(8,128)} %refs_7_.5, ...), custom_call_target="tpu_custom_call" | custom-call | tf_op jit(solution)/shard_map/pack_tiles/pallas_call | solution.py:51
  76.7 82.0 %all-gather.2.cloned.1.call-done = f32[16,4,32,128]{3,2,1,0:T(8,128)} async-done(((f32[1,4,32,128]{3,2,1,0:T(8,128)}), f32[16,4,32,128]{3,2,1,0:T(8,128)}) %all-gather.2.cloned.1.call-update) | async-done | bytes 1048592 | tf_op jit(solution)/shard_map/all_gather | solution.py:472
  159.1 8.7 %all-to-all-start.2 = ((f32[128,96,128]{2,1,0:T(8,128)}), f32[128,96,128]{2,1,0:T(8,128)}, u32[]{:S(2)}, u32[]{:S(2)}) async-start(f32[128,96,128]{2,1,0:T(8,128)} %pack_tiles.5), calls=%async_computation.2 | async-start | bytes 12582912 | tf_op jit(solution)/shard_map/all_to_all | solution.py:454
  167.8 3.4 collective-permute-start.1
  171.8 22.1 %add_pieces.2.refs_0_ = f32[6144,2,128]{2,1,0:T(2,128)} custom-call(s32[128,128]{1,0:T(8,128)} %copy-done.1, f32[128,56,2,128]{3,2,1,0:T(2,128)} %bitcast.13.pieces_ref, f32[128,12,2,128]{3,2,1,0:T(2,128)} %bitcast.53), custom_call_target="tpu_custom_call" | custom-call | flops 2147483648 | bytes 2147483648 | tf_op jit(solution)/shard_map/add_pieces/pallas_call | solution.py:98
  194.5 53.4 %collective-permute-done = f32[16,4,32,128]{3,2,1,0:T(8,128)S(1)} collective-permute-done((f32[16,4,32,128]{3,2,1,0:T(8,128)}, f32[16,4,32,128]{3,2,1,0:T(8,128)S(1)}, u32[]{:S(2)}, u32[]{:S(2)}) %collective-permute-start) | collective-permute-done | bytes 1048608 | tf_op jit(solution)/shard_map/ppermute | solution.py:483
  248.0 24.0 %collective-permute-done.1 = f32[16,4,32,128]{3,2,1,0:T(8,128)} collective-permute-done((f32[16,4,32,128]{3,2,1,0:T(8,128)S(1)}, f32[16,4,32,128]{3,2,1,0:T(8,128)}, u32[]{:S(2)}, u32[]{:S(2)}) %collective-permute-start.1) | collective-permute-done | bytes 1048608 | tf_op jit(solution)/shard_map/ppermute | solution.py:483
  272.1 1.3 bitcast_dynamic-update-slice_fusion.1
  273.4 2.4 copy.40
  275.8 11.6 %collective-permute-done.2 = f32[16,4,32,128]{3,2,1,0:T(8,128)S(1)} collective-permute-done((f32[16,4,32,128]{3,2,1,0:T(8,128)S(1)}, f32[16,4,32,128]{3,2,1,0:T(8,128)S(1)}, u32[]{:S(2)}, u32[]{:S(2)}) %collective-permute-start.2) | collective-permute-done | bytes 1048608 | tf_op jit(solution)/shard_map/ppermute | solution.py:483
  287.4 1.1 bitcast_dynamic-update-slice_fusion
  291.2 4.9 %collective-permute-done.3 = f32[16,4,4,32,128]{4,3,2,1,0:T(8,128)} collective-permute-done((f32[16,4,4,32,128]{4,3,2,1,0:T(8,128)}, f32[16,4,4,32,128]{4,3,2,1,0:T(8,128)}, u32[]{:S(2)}, u32[]{:S(2)}) %collective-permute-start.3) | collective-permute-done | bytes 4194336 | tf_op jit(solution)/shard_map/ppermute | solution.py:490
  296.1 3.4 broadcast_in_dim.121
  299.5 3.4 broadcast_in_dim.123
  302.9 1.8 copy_select_fusion
  304.6 26.0 %factor_corner.1 = (f32[512,512]{1,0:T(8,128)}, f32[512,512]{1,0:T(8,128)}) custom-call(f32[128,16,128]{2,1,0:T(8,128)} %bitcast.58, f32[8,128]{1,0:T(8,128)} %slice.25.diag_ref), custom_call_target="tpu_custom_call" | custom-call | tf_op jit(solution)/shard_map/factor_corner/pallas_call | solution.py:261
  330.6 0.8 constant_dynamic-slice_fusion
  332.1 5.9 %bitcast_select_fusion.top_ref = f32[128,4,32,128]{3,2,1,0:T(8,128)} fusion(f32[16,4,4,32,128]{4,3,2,1,0:T(8,128)} %collective-permute-done.3, f32[16,4,4,32,128]{4,3,2,1,0:T(8,128)} %bitcast_dynamic-update-slice_fusion, pred[128]{0:T(512)(128)(4,1)S(1)} %broadcast_in_dim.114), kind=kLoop, calls=%fused_computation | loop fusion | flops 2097152 | bytes 16777344 | tf_op jit(solution)/shard_map/jit(_where)/select_n | solution.py:491
  338.0 20.1 %add_pieces.3 = f32[6144,2,128]{2,1,0:T(2,128)} custom-call(s32[128,128]{1,0:T(8,128)} %copy-done.1, f32[128,48,2,128]{3,2,1,0:T(2,128)} %bitcast.20.pieces_ref, f32[6144,2,128]{2,1,0:T(2,128)} %add_pieces.2.refs_0_), custom_call_target="tpu_custom_call" | custom-call | flops 2147483648 | bytes 2147483648 | tf_op jit(solution)/shard_map/add_pieces/pallas_call | solution.py:98
  358.1 22.8 %update_rows.1 = f32[16,8,96,128]{3,2,1,0:T(8,128)} custom-call(f32[2,8,2,384,128]{4,3,2,1,0:T(8,128)} %bitcast.47, f32[2,8,2,384,128]{4,3,2,1,0:T(8,128)} %bitcast.48, f32[128,4,32,128]{3,2,1,0:T(8,128)} %bitcast_select_fusion.top_ref, f32[512,512]{1,0:T(8,128)} %get-tuple-element.27.inverse_ref, f32[8,512]{1,0:T(8,128)} %pad.9.own_ref, ...), custom_call_target="tpu_custom_call" | custom-call | tf_op jit(solution)/shard_map/update_rows/pallas_call | solution.py:358
  380.9 82.1 %all_to_all.20 = f32[128,96,128]{2,1,0:T(8,128)} all-to-all(f32[128,96,128]{2,1,0:T(8,128)} %bitcast.55), channel_id=1, replica_groups=mesh['row'=16,'col'=8] {'row','col'}, dimensions={0} | all-to-all | bytes 12582912 | tf_op jit(solution)/shard_map/all_to_all | solution.py:454
  463.0 9.6 %place_rows.1 = f32[24,128,4,128]{3,2,1,0:T(4,128)} custom-call(f32[128,24,4,128]{3,2,1,0:T(4,128)} %bitcast.54), custom_call_target="tpu_custom_call" | custom-call | tf_op jit(solution)/shard_map/place_rows/pallas_call | solution.py:391
  (42 shorter events, 9.1 us)
Async XLA Ops:
  18.8 36.4 %all-to-all-start = ((f32[128,24,128]{2,1,0:T(8,128)}), f32[128,24,128]{2,1,0:T(8,128)S(1)}, u32[]{:S(2)}, u32[]{:S(2)}) async-start(f32[128,24,128]{2,1,0:T(8,128)} %pack_tiles.3), calls=%async_computation | async-start | bytes 3145728 | tf_op jit(solution)/shard_map/all_to_all | solution.py:454
  55.2 5.8 %copy-start = (f32[128,24,128]{2,1,0:T(8,128)}, f32[128,24,128]{2,1,0:T(8,128)S(1)}, u32[]{:S(2)}) copy-start(f32[128,24,128]{2,1,0:T(8,128)S(1)} %all-to-all-done) | copy-start | bytes 4718596
  55.2 103.4 %all-to-all-start.1 = ((f32[128,112,128]{2,1,0:T(8,128)}), f32[128,112,128]{2,1,0:T(8,128)}, u32[]{:S(2)}, u32[]{:S(2)}) async-start(f32[128,112,128]{2,1,0:T(8,128)} %pack_tiles.4), calls=%async_computation.1 | async-start | bytes 14680064 | tf_op jit(solution)/shard_map/all_to_all | solution.py:454
  60.9 97.7 %all-gather.2.cloned.1.call-start = ((), (), s32[]{:S(2)}) async-start(), calls=%async_computation.4 | async-start | bytes 1114112 | tf_op jit(solution)/shard_map/all_gather | solution.py:472
  61.3 15.3 %copy-start.1 = (s32[128,128]{1,0:T(8,128)}, s32[128,128]{1,0:T(8,128)S(1)}, u32[]{:S(2)}) copy-start(s32[128,128]{1,0:T(8,128)S(1)} %fusion.5.target_ref) | copy-start | bytes 196612
  158.7 9.1 %copy-start.2 = (f32[16,4,32,128]{3,2,1,0:T(8,128)S(1)}, f32[16,4,32,128]{3,2,1,0:T(8,128)}, u32[]{:S(2)}) copy-start(f32[16,4,32,128]{3,2,1,0:T(8,128)} %all-gather.2.cloned.1.call-done) | copy-start | bytes 3145732
  158.7 89.3 %collective-permute-start = (f32[16,4,32,128]{3,2,1,0:T(8,128)}, f32[16,4,32,128]{3,2,1,0:T(8,128)S(1)}, u32[]{:S(2)}, u32[]{:S(2)}) collective-permute-start(f32[16,4,32,128]{3,2,1,0:T(8,128)} %all-gather.2.cloned.1.call-done), channel_id=1, source_target_pairs={{0,2},{1,3},{2,4},{3,5},{4,6},{5,7},{6,0},{7,1},{8,10},{9,11},{10,... | collective-permute-start | bytes 3145736 | tf_op jit(solution)/shard_map/ppermute | solution.py:483
  159.1 178.9 %all-to-all-start.2 = ((f32[128,96,128]{2,1,0:T(8,128)}), f32[128,96,128]{2,1,0:T(8,128)}, u32[]{:S(2)}, u32[]{:S(2)}) async-start(f32[128,96,128]{2,1,0:T(8,128)} %pack_tiles.5), calls=%async_computation.2 | async-start | bytes 12582912 | tf_op jit(solution)/shard_map/all_to_all | solution.py:454
  167.8 104.3 %collective-permute-start.1 = (f32[16,4,32,128]{3,2,1,0:T(8,128)S(1)}, f32[16,4,32,128]{3,2,1,0:T(8,128)}, u32[]{:S(2)}, u32[]{:S(2)}) collective-permute-start(f32[16,4,32,128]{3,2,1,0:T(8,128)S(1)} %copy-done.2), channel_id=1, source_target_pairs={{0,4},{1,5},{2,6},{3,7},{4,0},{5,1},{6,2},{7,3},{8,12},{9,13},{10,... | collective-permute-start | bytes 3145736 | tf_op jit(solution)/shard_map/ppermute | solution.py:483
  171.2 116.3 %collective-permute-start.2 = (f32[16,4,32,128]{3,2,1,0:T(8,128)S(1)}, f32[16,4,32,128]{3,2,1,0:T(8,128)S(1)}, u32[]{:S(2)}, u32[]{:S(2)}) collective-permute-start(f32[16,4,32,128]{3,2,1,0:T(8,128)S(1)} %copy-done.2), channel_id=1, source_target_pairs={{0,6},{1,7},{2,0},{3,1},{4,2},{5,3},{6,4},{7,5},{8,14},{9,15},{10,... | collective-permute-start | bytes 3145736 | tf_op jit(solution)/shard_map/ppermute | solution.py:483
  288.6 7.5 %collective-permute-start.3 = (f32[16,4,4,32,128]{4,3,2,1,0:T(8,128)}, f32[16,4,4,32,128]{4,3,2,1,0:T(8,128)}, u32[]{:S(2)}, u32[]{:S(2)}) collective-permute-start(f32[16,4,4,32,128]{4,3,2,1,0:T(8,128)} %bitcast_dynamic-update-slice_fusion), channel_id=1, source_target_pairs={{0,1},{1,0},{2,3},{3,2},{4,5},{5,4},{6,7},{7,6},{8,9},{9,8},{10,11... | collective-permute-start | bytes 12582920 | tf_op jit(solution)/shard_map/ppermute | solution.py:490
Sparse Core Ops, SparseCore 0:
  67.5 91.0 all-gather.1

commit v3 on v2

--- a/solution.py
+++ b/solution.py
@@ -267,9 +267,10 @@
     )(corner, diagonal)
 
 
-def update_rows(sums, top, inverse, own_rows, diagonal):
+def update_rows(core, sums, top, other_top, inverse, own_rows, diagonal):
     blocks, n_col, halves, n_rows, lanes = sums.shape
-    stripes, top_cols, _, _ = top.shape
+    pairs, top_cols, _, _ = top.shape
+    stripes = 2 * pairs
     near = top_cols * lanes
     n_row = stripes // n_col
     share = n_rows // 2 // n_row
@@ -280,9 +281,11 @@
         return lax.dot_general(a, b, dims, precision=HIGHEST, preferred_element_type=jnp.float32)
 
     def body(
+        core_ref,
         sums_ref,
         panel_in_ref,
         top_ref,
+        other_ref,
         inverse_ref,
         own_ref,
         diag_ref,
@@ -313,7 +316,11 @@
             panel_ref[...] = panel
             factor_ref[...] = dot(panel, inverse_ref[...], False)
 
-        flat_ref[...] = top_ref[...].reshape(stripes * top_cols * 8, lanes)
+        mine, theirs = top_ref[...], other_ref[...]
+        first = core_ref[0] == 0
+        both = [jnp.where(first, mine, theirs), jnp.where(first, theirs, mine)]
+        both = [x.reshape(pairs, 1, top_cols * 8, lanes) for x in both]
+        flat_ref[...] = jnp.concatenate(both, axis=1).reshape(stripes * top_cols * 8, lanes)
         for i in range(pair):
             c = g * pair + i
             for cb in range(blocks):
@@ -353,31 +360,40 @@
             out_ref[:, i] = mixed_ref[...].reshape(n_row, share * 8, lanes)
 
     def fixed(*shape):
-        return pl.BlockSpec(shape, lambda g: (0,) * len(shape))
-
+        return pl.BlockSpec(shape, lambda g, core_ref: (0,) * len(shape))
+
+    top_spec = pl.BlockSpec((pairs, top_cols, 8, lanes), lambda g, core_ref: (0, 0, g, 0))
     return pl.pallas_call(
         body,
-        grid=(n_col // pair,),
-        in_specs=[
-            pl.BlockSpec((blocks, pair, halves, n_rows, lanes), lambda g: (0, g, 0, 0, 0)),
-            pl.BlockSpec((1, 2, halves, n_rows, lanes), lambda g: (0, 0, 0, 0, 0)),
-            pl.BlockSpec((stripes, top_cols, 8, lanes), lambda g: (0, 0, g, 0)),
-            fixed(near, near),
-            fixed(8, near),
-            fixed(*diagonal.shape),
-        ],
-        out_specs=pl.BlockSpec((n_row, pair, share * 8, lanes), lambda g: (0, g, 0, 0)),
+        grid_spec=pltpu.PrefetchScalarGridSpec(
+            num_scalar_prefetch=1,
+            grid=(n_col // pair,),
+            in_specs=[
+                pl.BlockSpec(
+                    (blocks, pair, halves, n_rows, lanes), lambda g, core_ref: (0, g, 0, 0, 0)
+                ),
+                pl.BlockSpec((1, 2, halves, n_rows, lanes), lambda g, core_ref: (0, 0, 0, 0, 0)),
+                top_spec,
+                top_spec,
+                fixed(near, near),
+                fixed(8, near),
+                fixed(*diagonal.shape),
+            ],
+            out_specs=pl.BlockSpec(
+                (n_row, pair, share * 8, lanes), lambda g, core_ref: (0, g, 0, 0)
+            ),
+            scratch_shapes=[
+                pltpu.VMEM((n_rows, near), jnp.float32),
+                pltpu.VMEM((n_rows, near), jnp.float32),
+                pltpu.VMEM((stripes * top_cols * 8, lanes), jnp.float32),
+                pltpu.VMEM((n_rows, lanes), jnp.float32),
+                pltpu.VMEM((n_rows * 4, lanes), jnp.float32),
+            ],
+        ),
         out_shape=jax.ShapeDtypeStruct((n_row, n_col, share * 8, lanes), jnp.float32),
-        scratch_shapes=[
-            pltpu.VMEM((n_rows, near), jnp.float32),
-            pltpu.VMEM((n_rows, near), jnp.float32),
-            pltpu.VMEM((stripes * top_cols * 8, lanes), jnp.float32),
-            pltpu.VMEM((n_rows, lanes), jnp.float32),
-            pltpu.VMEM((n_rows * 4, lanes), jnp.float32),
-        ],
         compiler_params=pltpu.CompilerParams(vmem_limit_bytes=VMEM_BYTES),
         name="update_rows",
-    )(sums, sums, top, inverse, own_rows, diagonal)
+    )(core, sums, sums, top, other_top, inverse, own_rows, diagonal)
 
 
 def place_rows(received):
@@ -469,30 +485,40 @@
     spots = tile * top_rows + row % n_col * col_blocks + row // n_col
     spots = jnp.where(jnp.logical_and(tile < top_cols, row < top_rows), spots, n_top)
     view = add_top(spots, early, n_top)
-    share = lax.all_gather(view.reshape(top_cols, 2 * top_rows, lanes), "row")
-
-    second_pack = pack_tiles(order, child_tiles, mask_columns, at + CHUNKS[0], CHUNKS[1])
-    received0, second_pack, share = lax.optimization_barrier((received0, second_pack, share))
+    view = view.reshape(top_cols, 2 * top_rows, lanes)
     chips = n_col // 2
     my_chip, my_core = lax.axis_index("col") // 2, lax.axis_index("col") % 2
-    half_top = jnp.zeros((n_row, chips) + share.shape[1:], jnp.float32)
+    top = jnp.zeros((chips,) + view.shape, jnp.float32)
     for step in range(chips):
-        moved = share
+        moved = view
         if step:
             hops = [(2 * i + k, 2 * ((i + step) % chips) + k) for i in range(chips) for k in range(2)]
-            moved = lax.ppermute(share, "col", hops)
+            moved = lax.ppermute(view, "col", hops)
         origin = (my_chip + chips - step) % chips
-        half_top = lax.dynamic_update_slice(half_top, moved[:, None], (0, origin, 0, 0, 0))
+        top = lax.dynamic_update_slice(top, moved[None], (origin, 0, 0, 0))
+    corner = top.reshape(chips, top_cols, n_col, col_blocks, 2, lanes)[:, :, :2, 0]
+    corner = lax.all_gather(corner.reshape(chips, 4 * top_cols, lanes), "row")
+
+    second_pack = pack_tiles(order, child_tiles, mask_columns, at + CHUNKS[0], CHUNKS[1])
+    received0, second_pack, corner, top = lax.optimization_barrier(
+        (received0, second_pack, corner, top)
+    )
+
+    def from_other_core(x):
+        return lax.ppermute(x, "col", [(i, i + 1 - 2 * (i % 2)) for i in range(n_col)])
+
+    top = lax.all_gather(top, "row").reshape(devices // 2, top_cols, 2 * top_rows, lanes)
+    corner = corner.reshape(devices // 2, 1, 4 * top_cols, lanes)
+    other = from_other_core(corner)
+    corner = jnp.where(
+        my_core == 0,
+        jnp.concatenate([corner, other], axis=1),
+        jnp.concatenate([other, corner], axis=1),
+    )
     received1 = exchange(second_pack)
     pieces = received0.reshape(devices, CHUNKS[0], 2, lanes)
     sums = add_pieces(targets, pieces, early, None, at, BULK)
-    half_top, sums = lax.optimization_barrier((half_top, sums))
-    other_top = lax.ppermute(half_top, "col", [(i, i + 1 - 2 * (i % 2)) for i in range(n_col)])
-    top = jnp.where(
-        my_core == jnp.arange(2).reshape(1, 1, 2, 1, 1, 1), half_top[:, :, None], other_top[:, :, None]
-    )
-    top = top.reshape(devices, top_cols, 2 * top_rows, lanes)
-    corner = top.reshape(devices, top_cols, n_col, col_blocks, 2, lanes)[:, :, :2, 0]
+    corner, sums = lax.optimization_barrier((corner, sums))
     lower, inverse = factor_corner(corner.reshape(devices, 4 * top_cols, lanes), diagonal[:8])
     own_rows = lax.dynamic_slice(
         lower.reshape(top_cols, devices, top_cols * lanes),
@@ -500,13 +526,17 @@
         (top_cols, 1, top_cols * lanes),
     )
     own_rows = jnp.pad(own_rows.reshape(top_cols, top_cols * lanes), ((0, 8 - top_cols), (0, 0)))
-    received1, inverse, own_rows = lax.optimization_barrier((received1, inverse, own_rows))
+    received1, inverse, own_rows, top = lax.optimization_barrier(
+        (received1, inverse, own_rows, top)
+    )
+    other_top = from_other_core(top)
     pieces = received1.reshape(devices, CHUNKS[1], 2, lanes)
     sums = add_pieces(targets, pieces, None, sums, at + CHUNKS[0], BULK)
 
     own = jnp.where(jnp.arange(lanes, dtype=jnp.int32)[None, :] == me, diagonal, 0.0)
     result = update_rows(
-        sums.reshape(col_blocks, n_col, halves, 2 * row_tiles, lanes), top, inverse, own_rows, own
+        my_core.reshape(1),
+        sums.reshape(col_blocks, n_col, halves, 2 * row_tiles, lanes), top, other_top, inverse, own_rows, own
     )
     received = exchange(result.reshape(devices, -1, lanes))
     rows = place_rows(received)

time: 482 us -> 424 us (0.88)
  waiting for transfers between devices: 190 us -> 122 us
  blocking collectives: 82.1 us -> 102 us
  local copies, waits for them, and re-layouts: 18.2 us -> 8.63 us
  other arithmetic: 13.1 us -> 6.45 us
  starting transfers between devices: 30.8 us -> 36.5 us
    all_gather x1, waiting for transfers between devices: 82 us -> 12.9 us  [on_device(): lax.all_gather(top, 'row')]
    all_to_all x3, waiting for transfers between devices: 14.1 us -> 43.8 us  [exchange(): return lax.all_to_all(x, axes, split_axis=0, concat_axis=0, tiled=True)]
    ppermute x4 -> x5, waiting for transfers between devices: 93.9 us -> 65.4 us  [the longest x3 65.4 us: on_device(): moved = lax.ppermute(view, 'col', hops)]
    all_gather x0 -> x1, blocking collectives: none -> 20.7 us  [on_device(): corner = lax.all_gather(corner.reshape(chips, 4 * top_cols, lanes), 'row')]
    broadcast_in_dim x5 -> x1, local copies, waits for them, and re-layouts: 7.44 us -> 0.02 us  [on_device(): top = jnp.zeros((chips,) + view.shape, jnp.float32)]
    select_n x2 -> x1, other arithmetic: 7.69 us -> 1.06 us  [on_device(): jnp.where(my_core == 0, jnp.concatenate([corner, other], axis=1), jnp.con...]
  transfers between devices with their start and end apart: 8 -> 9, of which waited for: 6 -> 5; matrix products, arithmetic and copies ran while one was open for 5% -> 2% of each run, Pallas kernels for 15% -> 22%
where the time goes in v3:
time: 424 us; the launch traced here: 422 us
  Pallas kernels  130 us (31%)
  waiting for transfers between devices  122 us (29%)
  blocking collectives  102 us (24%)
  starting transfers between devices  36.5 us (9%)
  between operations  14.3 us (3%)
  local copies, waits for them, and re-layouts  8.63 us (2%)
  other arithmetic  6.45 us (2%)
    all_to_all x1, blocking collectives, exchange(): return lax.all_to_all(x, axes, split_axis=0, concat_axis=0, tiled=True)  81.4 us
    ppermute x3, waiting for transfers between devices, on_device(): moved = lax.ppermute(view, 'col', hops)  65.4 us
    all_to_all x3, waiting for transfers between devices, exchange(): return lax.all_to_all(x, axes, split_axis=0, concat_axis=0, tiled=True)  43.8 us
    pallas_call x2, Pallas kernels, add_pieces(): pl.pallas_call(body, grid_spec=pltpu.PrefetchScalarGridSpec(num_scalar_pr...  42.2 us
    all_to_all x3, starting transfers between devices, exchange(): return lax.all_to_all(x, axes, split_axis=0, concat_axis=0, tiled=True)  28.9 us
    pallas_call x1, Pallas kernels, factor_corner(): pl.pallas_call(body, out_shape=(shape, shape), scratch_shapes=[pltpu.VMEM...  26.1 us
    pallas_call x3, Pallas kernels, pack_tiles(): pl.pallas_call(body, grid_spec=pltpu.PrefetchScalarGridSpec(num_scalar_pr...  23.8 us
    pallas_call x1, Pallas kernels, update_rows(): pl.pallas_call(body, grid_spec=pltpu.PrefetchScalarGridSpec(num_scalar_pr...  23.2 us
  transfers between devices with their start and end apart: 9, of which 5 were waited for; matrix products, arithmetic and copies ran while one was open for 2% of the time, Pallas kernels for 22%

profile of v3, /device:TPU:1, one launch (start us, length us, event | category | flops | bytes accessed | tf_op | source)
XLA Modules:
  0.0 421.6 jit_solution(7697130056435194803)
XLA Ops:
  6.5 0.9 fusion.11
  7.5 0.9 fusion.15
  11.3 1.2 convolution_bitcast_fusion
  12.4 1.8 copy.26
  15.0 3.8 pack_tiles.3
  18.8 11.5 %all-to-all-start = ((f32[128,24,128]{2,1,0:T(8,128)}), f32[128,24,128]{2,1,0:T(8,128)S(1)}, u32[]{:S(2)}, u32[]{:S(2)}) async-start(f32[128,24,128]{2,1,0:T(8,128)} %pack_tiles.3), calls=%async_computation | async-start | bytes 3145728 | tf_op jit(solution)/shard_map/all_to_all | solution.py:470
  30.3 10.8 %pack_tiles.4 = f32[128,112,128]{2,1,0:T(8,128)} custom-call(s32[112]{0:T(128)} %get-tuple-element.34.order_ref, f32[112,256,128]{2,1,0:T(8,128)} %refs_7_.5, f32[112,256,128]{2,1,0:T(8,128)} %refs_7_.5, f32[112,256,128]{2,1,0:T(8,128)} %refs_7_.5, f32[112,256,128]{2,1,0:T(8,128)} %refs_7_.5, f32[112,256,128]{2,1,0:T(8,128)} %refs_7_.5, ...), custom_call_target="tpu_custom_call" | custom-call | tf_op jit(solution)/shard_map/pack_tiles/pallas_call | solution.py:51
  41.0 14.1 %all-to-all-done = f32[128,24,128]{2,1,0:T(8,128)S(1)} async-done(((f32[128,24,128]{2,1,0:T(8,128)}), f32[128,24,128]{2,1,0:T(8,128)S(1)}, u32[]{:S(2)}, u32[]{:S(2)}) %all-to-all-start) | async-done | bytes 1572896 | tf_op jit(solution)/shard_map/all_to_all | solution.py:470
  55.2 5.7 %all-to-all-start.1 = ((f32[128,112,128]{2,1,0:T(8,128)}), f32[128,112,128]{2,1,0:T(8,128)}, u32[]{:S(2)}, u32[]{:S(2)}) async-start(f32[128,112,128]{2,1,0:T(8,128)} %pack_tiles.4), calls=%async_computation.1 | async-start | bytes 14680064 | tf_op jit(solution)/shard_map/all_to_all | solution.py:470
  61.0 9.3 %pack_tiles.5 = f32[128,96,128]{2,1,0:T(8,128)} custom-call(s32[112]{0:T(128)} %get-tuple-element.34.order_ref, f32[112,256,128]{2,1,0:T(8,128)} %refs_7_.5, f32[112,256,128]{2,1,0:T(8,128)} %refs_7_.5, f32[112,256,128]{2,1,0:T(8,128)} %refs_7_.5, f32[112,256,128]{2,1,0:T(8,128)} %refs_7_.5, f32[112,256,128]{2,1,0:T(8,128)} %refs_7_.5, ...), custom_call_target="tpu_custom_call" | custom-call | tf_op jit(solution)/shard_map/pack_tiles/pallas_call | solution.py:51
  70.6 0.8 fusion.4.spot_ref
  71.4 5.3 %add_top.1 = f32[64,2,128]{2,1,0:T(2,128)} custom-call(s32[128,8]{1,0:T(8,128)} %fusion.4.spot_ref, f32[128,12,2,128]{3,2,1,0:T(2,128)} %bitcast.53), custom_call_target="tpu_custom_call" | custom-call | tf_op jit(solution)/shard_map/add_top/pallas_call | solution.py:133
  76.7 1.6 collective-permute-start
  78.3 2.9 collective-permute-start.1
  81.3 0.9 collective-permute-start.2
  82.2 0.9 constant_dynamic-update-slice_fusion
  83.1 33.1 %collective-permute-done = f32[4,32,128]{2,1,0:T(8,128)S(1)} collective-permute-done((f32[4,32,128]{2,1,0:T(8,128)}, f32[4,32,128]{2,1,0:T(8,128)S(1)}, u32[]{:S(2)}, u32[]{:S(2)}) %collective-permute-start) | collective-permute-done | bytes 65568 | tf_op jit(solution)/shard_map/ppermute | solution.py:496
  116.1 32.3 %collective-permute-done.1 = f32[4,32,128]{2,1,0:T(8,128)S(1)} collective-permute-done((f32[4,32,128]{2,1,0:T(8,128)}, f32[4,32,128]{2,1,0:T(8,128)S(1)}, u32[]{:S(2)}, u32[]{:S(2)}) %collective-permute-start.1) | collective-permute-done | bytes 65568 | tf_op jit(solution)/shard_map/ppermute | solution.py:496
  148.5 20.7 %all_gather.9 = f32[16,4,16,128]{3,2,1,0:T(8,128)S(1)} all-gather(f32[1,4,16,128]{3,2,1,0:T(8,128)S(1)} %bitcast.65), channel_id=1, replica_groups=mesh['row'=16,'col'=8] {'row'}, dimensions={0}, use_global_device_ids=true | all-gather | bytes 557056 | tf_op jit(solution)/shard_map/all_gather | solution.py:500
  169.3 11.7 %all-to-all-start.2 = ((f32[128,96,128]{2,1,0:T(8,128)}), f32[128,96,128]{2,1,0:T(8,128)}, u32[]{:S(2)}, u32[]{:S(2)}) async-start(f32[128,96,128]{2,1,0:T(8,128)} %pack_tiles.5), calls=%async_computation.2 | async-start | bytes 12582912 | tf_op jit(solution)/shard_map/all_to_all | solution.py:470
  181.0 1.4 collective-permute-start.3
  183.7 22.2 %add_pieces.2.refs_0_ = f32[6144,2,128]{2,1,0:T(2,128)} custom-call(s32[128,128]{1,0:T(8,128)} %copy-done.3, f32[128,56,2,128]{3,2,1,0:T(2,128)} %bitcast.19.pieces_ref, f32[128,12,2,128]{3,2,1,0:T(2,128)} %bitcast.54), custom_call_target="tpu_custom_call" | custom-call | flops 2147483648 | bytes 2147483648 | tf_op jit(solution)/shard_map/add_pieces/pallas_call | solution.py:98
  205.9 1.1 maximum_select_fusion
  207.0 26.1 %factor_corner.1 = (f32[512,512]{1,0:T(8,128)}, f32[512,512]{1,0:T(8,128)}) custom-call(f32[128,16,128]{2,1,0:T(8,128)} %bitcast.57, f32[8,128]{1,0:T(8,128)} %slice.24.diag_ref), custom_call_target="tpu_custom_call" | custom-call | tf_op jit(solution)/shard_map/factor_corner/pallas_call | solution.py:261
  233.0 0.8 constant_dynamic-slice_fusion
  234.5 29.7 %all-to-all-done.2 = f32[128,96,128]{2,1,0:T(8,128)} async-done(((f32[128,96,128]{2,1,0:T(8,128)}), f32[128,96,128]{2,1,0:T(8,128)}, u32[]{:S(2)}, u32[]{:S(2)}) %all-to-all-start.2) | async-done | bytes 6291488 | tf_op jit(solution)/shard_map/all_to_all | solution.py:470
  264.2 12.9 %all-gather.3.cloned.1.call-done.top_ref = f32[64,4,32,128]{3,2,1,0:T(8,128)} async-done(((f32[4,4,32,128]{3,2,1,0:T(8,128)}), f32[64,4,32,128]{3,2,1,0:T(8,128)}) %all-gather.3.cloned.1.call-update) | async-done | bytes 4194320 | tf_op jit(solution)/shard_map/all_gather | solution.py:510
  278.3 20.1 %add_pieces.3 = f32[6144,2,128]{2,1,0:T(2,128)} custom-call(s32[128,128]{1,0:T(8,128)} %copy-done.3, f32[128,48,2,128]{3,2,1,0:T(2,128)} %bitcast.24.pieces_ref, f32[6144,2,128]{2,1,0:T(2,128)} %add_pieces.2.refs_0_), custom_call_target="tpu_custom_call" | custom-call | flops 2147483648 | bytes 2147483648 | tf_op jit(solution)/shard_map/add_pieces/pallas_call | solution.py:98
  298.4 2.0 copy-done.1
  300.4 23.2 %update_rows.1 = f32[16,8,96,128]{3,2,1,0:T(8,128)} custom-call(s32[1]{0:T(128)} %bitcast.core_ref, f32[2,8,2,384,128]{4,3,2,1,0:T(8,128)} %bitcast.48, f32[2,8,2,384,128]{4,3,2,1,0:T(8,128)} %bitcast.49, f32[64,4,32,128]{3,2,1,0:T(8,128)} %all-gather.3.cloned.1.call-done.top_ref, f32[64,4,32,128]{3,2,1,0:T(8,128)} %copy-done.1, ...), custom_call_target="tpu_custom_call" | custom-call | tf_op jit(solution)/shard_map/update_rows/pallas_call | solution.py:366
  323.6 81.4 %all_to_all.20 = f32[128,96,128]{2,1,0:T(8,128)} all-to-all(f32[128,96,128]{2,1,0:T(8,128)} %bitcast.56), channel_id=1, replica_groups=mesh['row'=16,'col'=8] {'row','col'}, dimensions={0} | all-to-all | bytes 12582912 | tf_op jit(solution)/shard_map/all_to_all | solution.py:470
  405.1 9.6 %place_rows.1 = f32[24,128,4,128]{3,2,1,0:T(4,128)} custom-call(f32[128,24,4,128]{3,2,1,0:T(4,128)} %bitcast.55), custom_call_target="tpu_custom_call" | custom-call | tf_op jit(solution)/shard_map/place_rows/pallas_call | solution.py:407
  (41 shorter events, 6.6 us)
Async XLA Ops:
  18.8 36.4 %all-to-all-start = ((f32[128,24,128]{2,1,0:T(8,128)}), f32[128,24,128]{2,1,0:T(8,128)S(1)}, u32[]{:S(2)}, u32[]{:S(2)}) async-start(f32[128,24,128]{2,1,0:T(8,128)} %pack_tiles.3), calls=%async_computation | async-start | bytes 3145728 | tf_op jit(solution)/shard_map/all_to_all | solution.py:470
  55.2 15.1 %copy-start = (f32[128,24,128]{2,1,0:T(8,128)}, f32[128,24,128]{2,1,0:T(8,128)S(1)}, u32[]{:S(2)}) copy-start(f32[128,24,128]{2,1,0:T(8,128)S(1)} %all-to-all-done) | copy-start | bytes 4718596
  55.2 114.1 %all-to-all-start.1 = ((f32[128,112,128]{2,1,0:T(8,128)}), f32[128,112,128]{2,1,0:T(8,128)}, u32[]{:S(2)}, u32[]{:S(2)}) async-start(f32[128,112,128]{2,1,0:T(8,128)} %pack_tiles.4), calls=%async_computation.1 | async-start | bytes 14680064 | tf_op jit(solution)/shard_map/all_to_all | solution.py:470
  60.9 216.2 %all-gather.3.cloned.1.call-start = ((), (), s32[]{:S(2)}) async-start(), calls=%async_computation.4 | async-start | bytes 4456448 | tf_op jit(solution)/shard_map/all_gather | solution.py:510
  70.6 98.6 %copy-start.3 = (s32[128,128]{1,0:T(8,128)}, s32[128,128]{1,0:T(8,128)S(1)}, u32[]{:S(2)}) copy-start(s32[128,128]{1,0:T(8,128)S(1)} %fusion.5.target_ref) | copy-start | bytes 196612
  76.7 39.4 %collective-permute-start = (f32[4,32,128]{2,1,0:T(8,128)}, f32[4,32,128]{2,1,0:T(8,128)S(1)}, u32[]{:S(2)}, u32[]{:S(2)}) collective-permute-start(f32[4,32,128]{2,1,0:T(8,128)} %bitcast.61), channel_id=1, source_target_pairs={{0,2},{1,3},{2,4},{3,5},{4,6},{5,7},{6,0},{7,1},{8,10},{9,11},{10,... | collective-permute-start | bytes 196616 | tf_op jit(solution)/shard_map/ppermute | solution.py:496
  78.3 70.1 %collective-permute-start.1 = (f32[4,32,128]{2,1,0:T(8,128)}, f32[4,32,128]{2,1,0:T(8,128)S(1)}, u32[]{:S(2)}, u32[]{:S(2)}) collective-permute-start(f32[4,32,128]{2,1,0:T(8,128)} %bitcast.62), channel_id=1, source_target_pairs={{0,4},{1,5},{2,6},{3,7},{4,0},{5,1},{6,2},{7,3},{8,12},{9,13},{10,... | collective-permute-start | bytes 196616 | tf_op jit(solution)/shard_map/ppermute | solution.py:496
  81.3 67.2 %collective-permute-start.2 = (f32[4,32,128]{2,1,0:T(8,128)}, f32[4,32,128]{2,1,0:T(8,128)S(1)}, u32[]{:S(2)}, u32[]{:S(2)}) collective-permute-start(f32[4,32,128]{2,1,0:T(8,128)} %bitcast.63), channel_id=1, source_target_pairs={{0,6},{1,7},{2,0},{3,1},{4,2},{5,3},{6,4},{7,5},{8,14},{9,15},{10,... | collective-permute-start | bytes 196616 | tf_op jit(solution)/shard_map/ppermute | solution.py:496
  148.5 20.8 %copy-start.2 = (f32[4,4,32,128]{3,2,1,0:T(8,128)}, f32[4,4,32,128]{3,2,1,0:T(8,128)S(1)}, u32[]{:S(2)}) copy-start(f32[4,4,32,128]{3,2,1,0:T(8,128)S(1)} %bitcast_dynamic-update-slice_fusion) | copy-start | bytes 786436
  169.3 94.9 %all-to-all-start.2 = ((f32[128,96,128]{2,1,0:T(8,128)}), f32[128,96,128]{2,1,0:T(8,128)}, u32[]{:S(2)}, u32[]{:S(2)}) async-start(f32[128,96,128]{2,1,0:T(8,128)} %pack_tiles.5), calls=%async_computation.2 | async-start | bytes 12582912 | tf_op jit(solution)/shard_map/all_to_all | solution.py:470
  181.0 25.0 %collective-permute-start.3 = (f32[64,1,16,128]{3,2,1,0:T(8,128)S(1)}, f32[64,1,16,128]{3,2,1,0:T(8,128)S(1)}, u32[]{:S(2)}, u32[]{:S(2)}) collective-permute-start(f32[64,1,16,128]{3,2,1,0:T(8,128)S(1)} %bitcast.58), channel_id=1, source_target_pairs={{0,1},{1,0},{2,3},{3,2},{4,5},{5,4},{6,7},{7,6},{8,9},{9,8},{10,11... | collective-permute-start | bytes 1572872 | tf_op jit(solution)/shard_map/ppermute | solution.py:508
  277.1 21.3 %collective-permute-start.4 = (f32[64,4,32,128]{3,2,1,0:T(8,128)}, f32[64,4,32,128]{3,2,1,0:T(8,128)S(1)}, u32[]{:S(2)}, u32[]{:S(2)}) collective-permute-start(f32[64,4,32,128]{3,2,1,0:T(8,128)} %all-gather.3.cloned.1.call-done.top_ref), channel_id=1, source_target_pairs={{0,1},{1,0},{2,3},{3,2},{4,5},{5,4},{6,7},{7,6},{8,9},{9,8},{10,11... | collective-permute-start | bytes 12582920 | tf_op jit(solution)/shard_map/ppermute | solution.py:508
  298.4 2.0 copy-start.1
Sparse Core Ops, SparseCore 0:
  169.4 107.6 all-gather.2

commit v4 on v3

--- a/solution.py
+++ b/solution.py
@@ -8,7 +8,7 @@
 NF = 49152
 EARLY = 8
 GROUP = 8
-CHUNKS = (56, 48)
+CHUNKS = (64, 40)
 BULK = 2**31
 HIGHEST = lax.Precision.HIGHEST
 VMEM_BYTES = 56 * 1024 * 1024
@@ -473,7 +473,6 @@
     at = EARLY
     first_pack = pack_tiles(order, child_tiles, mask_columns, at, CHUNKS[0])
     early, first_pack = lax.optimization_barrier((early, first_pack))
-    received0 = exchange(first_pack)
 
     targets = early[:, 2 * EARLY, :].astype(jnp.int32)
     diagonal = early[:n_col, 2 * EARLY + 1 : 2 * EARLY + 1 + col_blocks * halves, :]
@@ -496,29 +495,26 @@
             moved = lax.ppermute(view, "col", hops)
         origin = (my_chip + chips - step) % chips
         top = lax.dynamic_update_slice(top, moved[None], (origin, 0, 0, 0))
-    corner = top.reshape(chips, top_cols, n_col, col_blocks, 2, lanes)[:, :, :2, 0]
-    corner = lax.all_gather(corner.reshape(chips, 4 * top_cols, lanes), "row")
+    top, first_pack = lax.optimization_barrier((top, first_pack))
+    received0 = exchange(first_pack)
+    top = lax.all_gather(top, "row").reshape(devices // 2, top_cols, 2 * top_rows, lanes)
 
     second_pack = pack_tiles(order, child_tiles, mask_columns, at + CHUNKS[0], CHUNKS[1])
-    received0, second_pack, corner, top = lax.optimization_barrier(
-        (received0, second_pack, corner, top)
-    )
-
-    def from_other_core(x):
-        return lax.ppermute(x, "col", [(i, i + 1 - 2 * (i % 2)) for i in range(n_col)])
-
-    top = lax.all_gather(top, "row").reshape(devices // 2, top_cols, 2 * top_rows, lanes)
-    corner = corner.reshape(devices // 2, 1, 4 * top_cols, lanes)
-    other = from_other_core(corner)
-    corner = jnp.where(
-        my_core == 0,
-        jnp.concatenate([corner, other], axis=1),
-        jnp.concatenate([other, corner], axis=1),
-    )
+    received0, second_pack = lax.optimization_barrier((received0, second_pack))
     received1 = exchange(second_pack)
     pieces = received0.reshape(devices, CHUNKS[0], 2, lanes)
     sums = add_pieces(targets, pieces, early, None, at, BULK)
-    corner, sums = lax.optimization_barrier((corner, sums))
+    top, sums = lax.optimization_barrier((top, sums))
+    swap = [(i, i + 1 - 2 * (i % 2)) for i in range(n_col)]
+    other_top = lax.ppermute(top, "col", swap)
+
+    def near_corner(x):
+        x = x.reshape(devices // 2, top_cols, n_col, col_blocks, 2, lanes)[:, :, :2, 0]
+        return x.reshape(devices // 2, 1, 4 * top_cols, lanes)
+
+    corner = jnp.where(
+        my_core == jnp.arange(2).reshape(1, 2, 1, 1), near_corner(top), near_corner(other_top)
+    )
     lower, inverse = factor_corner(corner.reshape(devices, 4 * top_cols, lanes), diagonal[:8])
     own_rows = lax.dynamic_slice(
         lower.reshape(top_cols, devices, top_cols * lanes),
@@ -526,10 +522,7 @@
         (top_cols, 1, top_cols * lanes),
     )
     own_rows = jnp.pad(own_rows.reshape(top_cols, top_cols * lanes), ((0, 8 - top_cols), (0, 0)))
-    received1, inverse, own_rows, top = lax.optimization_barrier(
-        (received1, inverse, own_rows, top)
-    )
-    other_top = from_other_core(top)
+    received1, inverse, own_rows = lax.optimization_barrier((received1, inverse, own_rows))
     pieces = received1.reshape(devices, CHUNKS[1], 2, lanes)
     sums = add_pieces(targets, pieces, None, sums, at + CHUNKS[0], BULK)
 

time: 424 us -> 405 us (0.955)
  blocking collectives: 102 us -> 82.6 us
  starting transfers between devices: 36.5 us -> 32.1 us
    all_to_all x3, waiting for transfers between devices: 43.8 us -> 119 us  [exchange(): return lax.all_to_all(x, axes, split_axis=0, concat_axis=0, tiled=True)]
    ppermute x3, waiting for transfers between devices: 65.4 us -> 2.53 us  [on_device(): moved = lax.ppermute(view, 'col', hops)]
    all_gather x1 -> x0, blocking collectives: 20.7 us -> none  [on_device(): corner = lax.all_gather(corner.reshape(chips, 4 * top_cols, lanes), 'row')]
    all_gather x1, waiting for transfers between devices: 12.9 us -> 0.01 us  [on_device(): lax.all_gather(top, 'row')]
  transfers between devices with their start and end apart: 9 -> 8, of which waited for: 5 -> 7; matrix products, arithmetic and copies ran while one was open for 2% -> 2% of each run, Pallas kernels for 22% -> 17%
where the time goes in v4:
time: 405 us; the launch traced here: 403 us
  Pallas kernels  130 us (32%)
  waiting for transfers between devices  125 us (31%)
  blocking collectives  82.6 us (20%)
  starting transfers between devices  32.1 us (8%)
  between operations  14.3 us (4%)
  local copies, waits for them, and re-layouts  9.93 us (2%)
  other arithmetic  6.69 us (2%)
    all_to_all x3, waiting for transfers between devices, exchange(): return lax.all_to_all(x, axes, split_axis=0, concat_axis=0, tiled=True)  119 us
    all_to_all x1, blocking collectives, exchange(): return lax.all_to_all(x, axes, split_axis=0, concat_axis=0, tiled=True)  82.6 us
    pallas_call x2, Pallas kernels, add_pieces(): pl.pallas_call(body, grid_spec=pltpu.PrefetchScalarGridSpec(num_scalar_pr...  42.1 us
    all_to_all x3, starting transfers between devices, exchange(): return lax.all_to_all(x, axes, split_axis=0, concat_axis=0, tiled=True)  28.3 us
    pallas_call x1, Pallas kernels, factor_corner(): pl.pallas_call(body, out_shape=(shape, shape), scratch_shapes=[pltpu.VMEM...  26 us
    pallas_call x3, Pallas kernels, pack_tiles(): pl.pallas_call(body, grid_spec=pltpu.PrefetchScalarGridSpec(num_scalar_pr...  24.1 us
    pallas_call x1, Pallas kernels, update_rows(): pl.pallas_call(body, grid_spec=pltpu.PrefetchScalarGridSpec(num_scalar_pr...  23.2 us
    pallas_call x1, Pallas kernels, place_rows(): pl.pallas_call(body, grid=(units // 2,), in_specs=[pl.BlockSpec((stripes,...  9.65 us
  transfers between devices with their start and end apart: 8, of which 7 were waited for; matrix products, arithmetic and copies ran while one was open for 2% of the time, Pallas kernels for 17%

profile of v4, /device:TPU:1, one launch (start us, length us, event | category | flops | bytes accessed | tf_op | source)
XLA Modules:
  0.0 402.5 jit_solution(7977606827299487592)
XLA Ops:
  6.5 0.9 fusion.11
  7.5 0.9 fusion.15
  11.3 1.2 convolution_bitcast_fusion
  12.4 1.8 copy.22
  15.0 3.9 pack_tiles.3
  18.8 11.5 %all-to-all-start = ((f32[128,24,128]{2,1,0:T(8,128)}), f32[128,24,128]{2,1,0:T(8,128)S(1)}, u32[]{:S(2)}, u32[]{:S(2)}) async-start(f32[128,24,128]{2,1,0:T(8,128)} %pack_tiles.3), calls=%async_computation | async-start | bytes 3145728 | tf_op jit(solution)/shard_map/all_to_all | solution.py:470
  30.4 11.7 %pack_tiles.4 = f32[128,128,128]{2,1,0:T(8,128)} custom-call(s32[112]{0:T(128)} %get-tuple-element.32.order_ref, f32[112,256,128]{2,1,0:T(8,128)} %refs_7_.5, f32[112,256,128]{2,1,0:T(8,128)} %refs_7_.5, f32[112,256,128]{2,1,0:T(8,128)} %refs_7_.5, f32[112,256,128]{2,1,0:T(8,128)} %refs_7_.5, f32[112,256,128]{2,1,0:T(8,128)} %refs_7_.5, ...), custom_call_target="tpu_custom_call" | custom-call | tf_op jit(solution)/shard_map/pack_tiles/pallas_call | solution.py:51
  42.0 13.2 %all-to-all-done = f32[128,24,128]{2,1,0:T(8,128)S(1)} async-done(((f32[128,24,128]{2,1,0:T(8,128)}), f32[128,24,128]{2,1,0:T(8,128)S(1)}, u32[]{:S(2)}, u32[]{:S(2)}) %all-to-all-start) | async-done | bytes 1572896 | tf_op jit(solution)/shard_map/all_to_all | solution.py:470
  55.6 0.9 fusion.4.spot_ref
  56.5 5.3 %add_top.1 = f32[64,2,128]{2,1,0:T(2,128)} custom-call(s32[128,8]{1,0:T(8,128)} %fusion.4.spot_ref, f32[128,12,2,128]{3,2,1,0:T(2,128)} %bitcast.51), custom_call_target="tpu_custom_call" | custom-call | tf_op jit(solution)/shard_map/add_top/pallas_call | solution.py:133
  61.7 1.0 collective-permute-start.1
  62.7 1.7 collective-permute-start.2
  64.4 0.9 constant_dynamic-update-slice_fusion
  65.3 1.4 collective-permute-done
  67.1 0.8 collective-permute-done.2
  68.5 7.0 %all-to-all-start.1 = ((f32[128,128,128]{2,1,0:T(8,128)}), f32[128,128,128]{2,1,0:T(8,128)}, u32[]{:S(2)}, u32[]{:S(2)}) async-start(f32[128,128,128]{2,1,0:T(8,128)} %pack_tiles.4), calls=%async_computation.1 | async-start | bytes 16777216 | tf_op jit(solution)/shard_map/all_to_all | solution.py:470
  76.3 8.5 %pack_tiles.5 = f32[128,80,128]{2,1,0:T(8,128)} custom-call(s32[112]{0:T(128)} %get-tuple-element.32.order_ref, f32[112,256,128]{2,1,0:T(8,128)} %refs_7_.5, f32[112,256,128]{2,1,0:T(8,128)} %refs_7_.5, f32[112,256,128]{2,1,0:T(8,128)} %refs_7_.5, f32[112,256,128]{2,1,0:T(8,128)} %refs_7_.5, f32[112,256,128]{2,1,0:T(8,128)} %refs_7_.5, ...), custom_call_target="tpu_custom_call" | custom-call | tf_op jit(solution)/shard_map/pack_tiles/pallas_call | solution.py:51
  84.9 102.6 %all-to-all-done.1 = f32[128,128,128]{2,1,0:T(8,128)} async-done(((f32[128,128,128]{2,1,0:T(8,128)}), f32[128,128,128]{2,1,0:T(8,128)}, u32[]{:S(2)}, u32[]{:S(2)}) %all-to-all-start.1) | async-done | bytes 8388640 | tf_op jit(solution)/shard_map/all_to_all | solution.py:470
  187.5 9.7 %all-to-all-start.2 = ((f32[128,80,128]{2,1,0:T(8,128)}), f32[128,80,128]{2,1,0:T(8,128)}, u32[]{:S(2)}, u32[]{:S(2)}) async-start(f32[128,80,128]{2,1,0:T(8,128)} %pack_tiles.5), calls=%async_computation.2 | async-start | bytes 10485760 | tf_op jit(solution)/shard_map/all_to_all | solution.py:470
  197.2 23.1 %add_pieces.2.refs_0_ = f32[6144,2,128]{2,1,0:T(2,128)} custom-call(s32[128,128]{1,0:T(8,128)} %copy-done.1, f32[128,64,2,128]{3,2,1,0:T(2,128)} %bitcast.13.pieces_ref, f32[128,12,2,128]{3,2,1,0:T(2,128)} %bitcast.52), custom_call_target="tpu_custom_call" | custom-call | flops 2147483648 | bytes 2147483648 | tf_op jit(solution)/shard_map/add_pieces/pallas_call | solution.py:98
  220.3 1.1 collective-permute-start.3
  223.7 1.3 slice.27
  224.9 3.7 collective-permute-done.3.other_ref
  228.6 1.3 slice.28
  229.8 1.2 bitcast_select_fusion.corner_ref
  231.0 26.0 %factor_corner.1 = (f32[512,512]{1,0:T(8,128)}, f32[512,512]{1,0:T(8,128)}) custom-call(f32[128,16,128]{2,1,0:T(8,128)} %bitcast_select_fusion.corner_ref, f32[8,128]{1,0:T(8,128)} %slice.29.diag_ref), custom_call_target="tpu_custom_call" | custom-call | tf_op jit(solution)/shard_map/factor_corner/pallas_call | solution.py:261
  257.0 0.8 constant_dynamic-slice_fusion
  258.5 2.8 all-to-all-done.2
  261.2 18.9 %add_pieces.3 = f32[6144,2,128]{2,1,0:T(2,128)} custom-call(s32[128,128]{1,0:T(8,128)} %copy-done.1, f32[128,40,2,128]{3,2,1,0:T(2,128)} %bitcast.23.pieces_ref, f32[6144,2,128]{2,1,0:T(2,128)} %add_pieces.2.refs_0_), custom_call_target="tpu_custom_call" | custom-call | flops 2147483648 | bytes 2147483648 | tf_op jit(solution)/shard_map/add_pieces/pallas_call | solution.py:98
  280.2 23.2 %update_rows.1 = f32[16,8,96,128]{3,2,1,0:T(8,128)} custom-call(s32[1]{0:T(128)} %bitcast.core_ref, f32[2,8,2,384,128]{4,3,2,1,0:T(8,128)} %bitcast.46, f32[2,8,2,384,128]{4,3,2,1,0:T(8,128)} %bitcast.47, f32[64,4,32,128]{3,2,1,0:T(8,128)} %all-gather.3.cloned.1.call-done.top_ref, f32[64,4,32,128]{3,2,1,0:T(8,128)} %collective-permute-done.3.other_ref, ...), custom_call_target="tpu_custom_call" | custom-call | tf_op jit(solution)/shard_map/update_rows/pallas_call | solution.py:366
  303.4 82.6 %all_to_all.20 = f32[128,96,128]{2,1,0:T(8,128)} all-to-all(f32[128,96,128]{2,1,0:T(8,128)} %bitcast.54), channel_id=1, replica_groups=mesh['row'=16,'col'=8] {'row','col'}, dimensions={0} | all-to-all | bytes 12582912 | tf_op jit(solution)/shard_map/all_to_all | solution.py:470
  386.0 9.6 %place_rows.1 = f32[24,128,4,128]{3,2,1,0:T(4,128)} custom-call(f32[128,24,4,128]{3,2,1,0:T(4,128)} %bitcast.53), custom_call_target="tpu_custom_call" | custom-call | tf_op jit(solution)/shard_map/place_rows/pallas_call | solution.py:407
  (40 shorter events, 7.8 us)
Async XLA Ops:
  18.8 36.4 %all-to-all-start = ((f32[128,24,128]{2,1,0:T(8,128)}), f32[128,24,128]{2,1,0:T(8,128)S(1)}, u32[]{:S(2)}, u32[]{:S(2)}) async-start(f32[128,24,128]{2,1,0:T(8,128)} %pack_tiles.3), calls=%async_computation | async-start | bytes 3145728 | tf_op jit(solution)/shard_map/all_to_all | solution.py:470
  55.2 1.2 copy-start
  55.6 12.3 %copy-start.1 = (s32[128,128]{1,0:T(8,128)}, s32[128,128]{1,0:T(8,128)S(1)}, u32[]{:S(2)}) copy-start(s32[128,128]{1,0:T(8,128)S(1)} %fusion.5.target_ref) | copy-start | bytes 196612
  61.7 4.9 %collective-permute-start = (f32[4,32,128]{2,1,0:T(8,128)}, f32[4,32,128]{2,1,0:T(8,128)S(1)}, u32[]{:S(2)}, u32[]{:S(2)}) collective-permute-start(f32[4,32,128]{2,1,0:T(8,128)} %bitcast.58), channel_id=1, source_target_pairs={{0,2},{1,3},{2,4},{3,5},{4,6},{5,7},{6,0},{7,1},{8,10},{9,11},{10,... | collective-permute-start | bytes 196616 | tf_op jit(solution)/shard_map/ppermute | solution.py:495
  61.7 5.3 %collective-permute-start.1 = (f32[4,32,128]{2,1,0:T(8,128)}, f32[4,32,128]{2,1,0:T(8,128)S(1)}, u32[]{:S(2)}, u32[]{:S(2)}) collective-permute-start(f32[4,32,128]{2,1,0:T(8,128)} %bitcast.59), channel_id=1, source_target_pairs={{0,4},{1,5},{2,6},{3,7},{4,0},{5,1},{6,2},{7,3},{8,12},{9,13},{10,... | collective-permute-start | bytes 196616 | tf_op jit(solution)/shard_map/ppermute | solution.py:495
  62.7 5.1 %collective-permute-start.2 = (f32[4,32,128]{2,1,0:T(8,128)}, f32[4,32,128]{2,1,0:T(8,128)S(1)}, u32[]{:S(2)}, u32[]{:S(2)}) collective-permute-start(f32[4,32,128]{2,1,0:T(8,128)} %bitcast.60), channel_id=1, source_target_pairs={{0,6},{1,7},{2,0},{3,1},{4,2},{5,3},{6,4},{7,5},{8,14},{9,15},{10,... | collective-permute-start | bytes 196616 | tf_op jit(solution)/shard_map/ppermute | solution.py:495
  67.9 0.7 copy-start.2
  68.5 118.9 %all-to-all-start.1 = ((f32[128,128,128]{2,1,0:T(8,128)}), f32[128,128,128]{2,1,0:T(8,128)}, u32[]{:S(2)}, u32[]{:S(2)}) async-start(f32[128,128,128]{2,1,0:T(8,128)} %pack_tiles.4), calls=%async_computation.1 | async-start | bytes 16777216 | tf_op jit(solution)/shard_map/all_to_all | solution.py:470
  75.6 144.8 %all-gather.3.cloned.1.call-start = ((), (), s32[]{:S(2)}) async-start(), calls=%async_computation.4 | async-start | bytes 4456448 | tf_op jit(solution)/shard_map/all_gather | solution.py:500
  187.5 73.8 %all-to-all-start.2 = ((f32[128,80,128]{2,1,0:T(8,128)}), f32[128,80,128]{2,1,0:T(8,128)}, u32[]{:S(2)}, u32[]{:S(2)}) async-start(f32[128,80,128]{2,1,0:T(8,128)} %pack_tiles.5), calls=%async_computation.2 | async-start | bytes 10485760 | tf_op jit(solution)/shard_map/all_to_all | solution.py:470
  220.3 8.3 %collective-permute-start.3 = (f32[64,4,32,128]{3,2,1,0:T(8,128)}, f32[64,4,32,128]{3,2,1,0:T(8,128)}, u32[]{:S(2)}, u32[]{:S(2)}) collective-permute-start(f32[64,4,32,128]{3,2,1,0:T(8,128)} %all-gather.3.cloned.1.call-done.top_ref), channel_id=1, source_target_pairs={{0,1},{1,0},{2,3},{3,2},{4,5},{5,4},{6,7},{7,6},{8,9},{9,8},{10,11... | collective-permute-start | bytes 12582920 | tf_op jit(solution)/shard_map/ppermute | solution.py:509
Sparse Core Ops, SparseCore 0:
  78.6 119.2 all-gather.2

commit v5 on v4

--- a/solution.py
+++ b/solution.py
@@ -8,7 +8,7 @@
 NF = 49152
 EARLY = 8
 GROUP = 8
-CHUNKS = (64, 40)
+CHUNKS = (72, 32)
 BULK = 2**31
 HIGHEST = lax.Precision.HIGHEST
 VMEM_BYTES = 56 * 1024 * 1024
@@ -63,7 +63,7 @@
     )(order, *operands)
 
 
-def add_pieces(targets, pieces, early, sums, first, weight):
+def add_pieces(targets, pieces, early, sums, first, window, weight):
     sources, count, two, lanes = pieces.shape
     n_sums = 6144
     per_step = 8
@@ -83,10 +83,10 @@
                 for i in range(EARLY):
                     d = target_ref[source, i]
                     sums_ref[d] = sums_ref[d] + refs[0][n, i]
-            for at in range(0, count, GROUP):
-                ds = [target_ref[source, first + at + i] for i in range(GROUP)]
-                news = [sums_ref[ds[i]] + pieces_ref[n, at + i] for i in range(GROUP)]
-                for i in range(GROUP):
+            for at in range(0, count, window):
+                ds = [target_ref[source, first + at + i] for i in range(window)]
+                news = [sums_ref[ds[i]] + pieces_ref[n, at + i] for i in range(window)]
+                for i in range(window):
                     sums_ref[ds[i]] = news[i]
 
     def streamed(x):
@@ -278,7 +278,8 @@
 
     def dot(a, b, transposed):
         dims = (((1,), (1 if transposed else 0,)), ((), ()))
-        return lax.dot_general(a, b, dims, precision=HIGHEST, preferred_element_type=jnp.float32)
+        precision = HIGHEST if a.dtype == jnp.float32 else None
+        return lax.dot_general(a, b, dims, precision=precision, preferred_element_type=jnp.float32)
 
     def body(
         core_ref,
@@ -291,7 +292,8 @@
         diag_ref,
         out_ref,
         panel_ref,
-        factor_ref,
+        high_ref,
+        low_ref,
         flat_ref,
         result_ref,
         mixed_ref,
@@ -314,7 +316,9 @@
             head = jnp.where(at < 4, own_ref[...], panel[:8])
             panel = jnp.concatenate([head, panel[8:]], axis=0)
             panel_ref[...] = panel
-            factor_ref[...] = dot(panel, inverse_ref[...], False)
+            factor = dot(panel, inverse_ref[...], False)
+            high_ref[...] = factor.astype(jnp.bfloat16)
+            low_ref[...] = (factor - high_ref[...].astype(jnp.float32)).astype(jnp.bfloat16)
 
         mine, theirs = top_ref[...], other_ref[...]
         first = core_ref[0] == 0
@@ -344,7 +348,10 @@
                     ],
                     axis=0,
                 )
-                product = dot(factor_ref[...], weights, True)
+                high = weights.astype(jnp.bfloat16)
+                low = (weights - high.astype(jnp.float32)).astype(jnp.bfloat16)
+                product = dot(low_ref[...], high, True) + dot(high_ref[...], low, True)
+                product = product + dot(high_ref[...], high, True)
                 for h in range(halves):
                     t = (cb * n_col + c) * halves + h
                     result = with_diagonal(sums_ref[cb, i, h], t)
@@ -384,7 +391,8 @@
             ),
             scratch_shapes=[
                 pltpu.VMEM((n_rows, near), jnp.float32),
-                pltpu.VMEM((n_rows, near), jnp.float32),
+                pltpu.VMEM((n_rows, near), jnp.bfloat16),
+                pltpu.VMEM((n_rows, near), jnp.bfloat16),
                 pltpu.VMEM((stripes * top_cols * 8, lanes), jnp.float32),
                 pltpu.VMEM((n_rows, lanes), jnp.float32),
                 pltpu.VMEM((n_rows * 4, lanes), jnp.float32),
@@ -399,16 +407,17 @@
 def place_rows(received):
     stripes, width, lanes = received.shape
     units = width // 4
+    share = units // 2
 
     def body(in_ref, out_ref):
-        for s in range(2):
+        for s in range(share):
             out_ref[s] = in_ref[:, s]
 
     return pl.pallas_call(
         body,
-        grid=(units // 2,),
-        in_specs=[pl.BlockSpec((stripes, 2, 4, lanes), lambda g: (0, g, 0, 0))],
-        out_specs=pl.BlockSpec((2, stripes, 4, lanes), lambda g: (g, 0, 0, 0)),
+        grid=(units // share,),
+        in_specs=[pl.BlockSpec((stripes, share, 4, lanes), lambda g: (0, g, 0, 0))],
+        out_specs=pl.BlockSpec((share, stripes, 4, lanes), lambda g: (g, 0, 0, 0)),
         out_shape=jax.ShapeDtypeStruct((units, stripes, 4, lanes), jnp.float32),
         compiler_params=pltpu.CompilerParams(vmem_limit_bytes=VMEM_BYTES),
         name="place_rows",
@@ -503,7 +512,7 @@
     received0, second_pack = lax.optimization_barrier((received0, second_pack))
     received1 = exchange(second_pack)
     pieces = received0.reshape(devices, CHUNKS[0], 2, lanes)
-    sums = add_pieces(targets, pieces, early, None, at, BULK)
+    sums = add_pieces(targets, pieces, early, None, at, 12, BULK)
     top, sums = lax.optimization_barrier((top, sums))
     swap = [(i, i + 1 - 2 * (i % 2)) for i in range(n_col)]
     other_top = lax.ppermute(top, "col", swap)
@@ -524,7 +533,7 @@
     own_rows = jnp.pad(own_rows.reshape(top_cols, top_cols * lanes), ((0, 8 - top_cols), (0, 0)))
     received1, inverse, own_rows = lax.optimization_barrier((received1, inverse, own_rows))
     pieces = received1.reshape(devices, CHUNKS[1], 2, lanes)
-    sums = add_pieces(targets, pieces, None, sums, at + CHUNKS[0], BULK)
+    sums = add_pieces(targets, pieces, None, sums, at + CHUNKS[0], 16, BULK)
 
     own = jnp.where(jnp.arange(lanes, dtype=jnp.int32)[None, :] == me, diagonal, 0.0)
     result = update_rows(

time: 405 us -> 423 us (1.044)
  waiting for transfers between devices: 125 us -> 155 us
  Pallas kernels: 130 us -> 121 us
    all_to_all x3, waiting for transfers between devices: 119 us -> 151 us  [exchange(): return lax.all_to_all(x, axes, split_axis=0, concat_axis=0, tiled=True)]
    pallas_call x1, Pallas kernels: 23.2 us -> 18.2 us  [update_rows(): pl.pallas_call(body, grid_spec=pltpu.PrefetchScalarGridSpec(num_scalar_pr...]
    pallas_call x1, Pallas kernels: 9.65 us -> 5.15 us  [place_rows(): pl.pallas_call(body, grid=(units // share,), in_specs=[pl.BlockSpec((stri...]
  transfers between devices with their start and end apart: 8 -> 8, of which waited for: 7 -> 6; matrix products, arithmetic and copies ran while one was open for 2% -> 2% of each run, Pallas kernels for 17% -> 17%
where the time goes in v5:
time: 423 us; the launch traced here: 421 us
  waiting for transfers between devices  155 us (37%)
  Pallas kernels  121 us (29%)
  blocking collectives  81.2 us (19%)
  starting transfers between devices  32.4 us (8%)
  between operations  14.3 us (3%)
  local copies, waits for them, and re-layouts  9.96 us (2%)
  other arithmetic  6.67 us (2%)
    all_to_all x3, waiting for transfers between devices, exchange(): return lax.all_to_all(x, axes, split_axis=0, concat_axis=0, tiled=True)  151 us
    all_to_all x1, blocking collectives, exchange(): return lax.all_to_all(x, axes, split_axis=0, concat_axis=0, tiled=True)  81.2 us
    pallas_call x2, Pallas kernels, add_pieces(): pl.pallas_call(body, grid_spec=pltpu.PrefetchScalarGridSpec(num_scalar_pr...  42.6 us
    all_to_all x3, starting transfers between devices, exchange(): return lax.all_to_all(x, axes, split_axis=0, concat_axis=0, tiled=True)  27.9 us
    pallas_call x1, Pallas kernels, factor_corner(): pl.pallas_call(body, out_shape=(shape, shape), scratch_shapes=[pltpu.VMEM...  26 us
    pallas_call x3, Pallas kernels, pack_tiles(): pl.pallas_call(body, grid_spec=pltpu.PrefetchScalarGridSpec(num_scalar_pr...  23.9 us
    pallas_call x1, Pallas kernels, update_rows(): pl.pallas_call(body, grid_spec=pltpu.PrefetchScalarGridSpec(num_scalar_pr...  18.2 us
  transfers between devices with their start and end apart: 8, of which 6 were waited for; matrix products, arithmetic and copies ran while one was open for 2% of the time, Pallas kernels for 17%

profile of v5, /device:TPU:1, one launch (start us, length us, event | category | flops | bytes accessed | tf_op | source)
XLA Modules:
  0.0 421.3 jit_solution(1978288432353774285)
XLA Ops:
  6.5 0.9 fusion.11
  7.5 0.9 fusion.15
  11.3 1.2 convolution_bitcast_fusion
  12.4 1.8 copy.22
  15.0 3.8 pack_tiles.3
  18.8 11.5 %all-to-all-start = ((f32[128,24,128]{2,1,0:T(8,128)}), f32[128,24,128]{2,1,0:T(8,128)S(1)}, u32[]{:S(2)}, u32[]{:S(2)}) async-start(f32[128,24,128]{2,1,0:T(8,128)} %pack_tiles.3), calls=%async_computation | async-start | bytes 3145728 | tf_op jit(solution)/shard_map/all_to_all | solution.py:479
  30.3 13.0 %pack_tiles.4 = f32[128,144,128]{2,1,0:T(8,128)} custom-call(s32[112]{0:T(128)} %get-tuple-element.32.order_ref, f32[112,256,128]{2,1,0:T(8,128)} %refs_7_.5, f32[112,256,128]{2,1,0:T(8,128)} %refs_7_.5, f32[112,256,128]{2,1,0:T(8,128)} %refs_7_.5, f32[112,256,128]{2,1,0:T(8,128)} %refs_7_.5, f32[112,256,128]{2,1,0:T(8,128)} %refs_7_.5, ...), custom_call_target="tpu_custom_call" | custom-call | tf_op jit(solution)/shard_map/pack_tiles/pallas_call | solution.py:51
  43.4 11.8 %all-to-all-done = f32[128,24,128]{2,1,0:T(8,128)S(1)} async-done(((f32[128,24,128]{2,1,0:T(8,128)}), f32[128,24,128]{2,1,0:T(8,128)S(1)}, u32[]{:S(2)}, u32[]{:S(2)}) %all-to-all-start) | async-done | bytes 1572896 | tf_op jit(solution)/shard_map/all_to_all | solution.py:479
  55.5 0.9 fusion.4.spot_ref
  56.4 5.3 %add_top.1 = f32[64,2,128]{2,1,0:T(2,128)} custom-call(s32[128,8]{1,0:T(8,128)} %fusion.4.spot_ref, f32[128,12,2,128]{3,2,1,0:T(2,128)} %bitcast.51), custom_call_target="tpu_custom_call" | custom-call | tf_op jit(solution)/shard_map/add_top/pallas_call | solution.py:133
  61.6 1.0 collective-permute-start.1
  62.6 1.7 collective-permute-start.2
  64.3 0.9 constant_dynamic-update-slice_fusion
  65.2 1.4 collective-permute-done
  67.0 0.8 collective-permute-done.2
  68.5 7.0 %all-to-all-start.1 = ((f32[128,144,128]{2,1,0:T(8,128)}), f32[128,144,128]{2,1,0:T(8,128)}, u32[]{:S(2)}, u32[]{:S(2)}) async-start(f32[128,144,128]{2,1,0:T(8,128)} %pack_tiles.4), calls=%async_computation.1 | async-start | bytes 18874368 | tf_op jit(solution)/shard_map/all_to_all | solution.py:479
  76.2 7.0 %pack_tiles.5 = f32[128,64,128]{2,1,0:T(8,128)} custom-call(s32[112]{0:T(128)} %get-tuple-element.32.order_ref, f32[112,256,128]{2,1,0:T(8,128)} %refs_7_.5, f32[112,256,128]{2,1,0:T(8,128)} %refs_7_.5, f32[112,256,128]{2,1,0:T(8,128)} %refs_7_.5, f32[112,256,128]{2,1,0:T(8,128)} %refs_7_.5, f32[112,256,128]{2,1,0:T(8,128)} %refs_7_.5, ...), custom_call_target="tpu_custom_call" | custom-call | tf_op jit(solution)/shard_map/pack_tiles/pallas_call | solution.py:51
  83.2 120.1 %all-to-all-done.1 = f32[128,144,128]{2,1,0:T(8,128)} async-done(((f32[128,144,128]{2,1,0:T(8,128)}), f32[128,144,128]{2,1,0:T(8,128)}, u32[]{:S(2)}, u32[]{:S(2)}) %all-to-all-start.1) | async-done | bytes 9437216 | tf_op jit(solution)/shard_map/all_to_all | solution.py:479
  203.3 25.1 %add_pieces.2.refs_0_ = f32[6144,2,128]{2,1,0:T(2,128)} custom-call(s32[128,128]{1,0:T(8,128)} %copy-done.1, f32[128,72,2,128]{3,2,1,0:T(2,128)} %bitcast.13.pieces_ref, f32[128,12,2,128]{3,2,1,0:T(2,128)} %bitcast.52), custom_call_target="tpu_custom_call" | custom-call | flops 2147483648 | bytes 2147483648 | tf_op jit(solution)/shard_map/add_pieces/pallas_call | solution.py:98
  228.4 1.8 collective-permute-start.3
  230.2 9.4 %all-to-all-start.2 = ((f32[128,64,128]{2,1,0:T(8,128)}), f32[128,64,128]{2,1,0:T(8,128)}, u32[]{:S(2)}, u32[]{:S(2)}) async-start(f32[128,64,128]{2,1,0:T(8,128)} %pack_tiles.5), calls=%async_computation.2 | async-start | bytes 8388608 | tf_op jit(solution)/shard_map/all_to_all | solution.py:479
  239.8 0.8 slice.23
  241.8 1.3 slice.27
  243.1 1.3 slice.28
  244.3 1.2 bitcast_select_fusion.corner_ref
  245.5 26.0 %factor_corner.1 = (f32[512,512]{1,0:T(8,128)}, f32[512,512]{1,0:T(8,128)}) custom-call(f32[128,16,128]{2,1,0:T(8,128)} %bitcast_select_fusion.corner_ref, f32[8,128]{1,0:T(8,128)} %slice.29.diag_ref), custom_call_target="tpu_custom_call" | custom-call | tf_op jit(solution)/shard_map/factor_corner/pallas_call | solution.py:261
  271.5 0.8 constant_dynamic-slice_fusion
  273.0 19.4 %all-to-all-done.2 = f32[128,64,128]{2,1,0:T(8,128)} async-done(((f32[128,64,128]{2,1,0:T(8,128)}), f32[128,64,128]{2,1,0:T(8,128)}, u32[]{:S(2)}, u32[]{:S(2)}) %all-to-all-start.2) | async-done | bytes 4194336 | tf_op jit(solution)/shard_map/all_to_all | solution.py:479
  292.4 17.5 %add_pieces.3 = f32[6144,2,128]{2,1,0:T(2,128)} custom-call(s32[128,128]{1,0:T(8,128)} %copy-done.1, f32[128,32,2,128]{3,2,1,0:T(2,128)} %bitcast.23.pieces_ref, f32[6144,2,128]{2,1,0:T(2,128)} %add_pieces.2.refs_0_), custom_call_target="tpu_custom_call" | custom-call | flops 2147483648 | bytes 2147483648 | tf_op jit(solution)/shard_map/add_pieces/pallas_call | solution.py:98
  309.9 18.2 %update_rows.1 = f32[16,8,96,128]{3,2,1,0:T(8,128)} custom-call(s32[1]{0:T(128)} %bitcast.core_ref, f32[2,8,2,384,128]{4,3,2,1,0:T(8,128)} %bitcast.46, f32[2,8,2,384,128]{4,3,2,1,0:T(8,128)} %bitcast.47, f32[64,4,32,128]{3,2,1,0:T(8,128)} %all-gather.3.cloned.1.call-done.top_ref, f32[64,4,32,128]{3,2,1,0:T(8,128)} %collective-permute-done.3.other_ref, ...), custom_call_target="tpu_custom_call" | custom-call | tf_op jit(solution)/shard_map/update_rows/pallas_call | solution.py:373
  328.1 81.2 %all_to_all.20 = f32[128,96,128]{2,1,0:T(8,128)} all-to-all(f32[128,96,128]{2,1,0:T(8,128)} %bitcast.54), channel_id=1, replica_groups=mesh['row'=16,'col'=8] {'row','col'}, dimensions={0} | all-to-all | bytes 12582912 | tf_op jit(solution)/shard_map/all_to_all | solution.py:479
  409.3 5.1 %place_rows.1 = f32[24,128,4,128]{3,2,1,0:T(4,128)} custom-call(f32[128,24,4,128]{3,2,1,0:T(4,128)} %bitcast.53), custom_call_target="tpu_custom_call" | custom-call | tf_op jit(solution)/shard_map/place_rows/pallas_call | solution.py:416
  (40 shorter events, 7.1 us)
Async XLA Ops:
  18.8 36.4 %all-to-all-start = ((f32[128,24,128]{2,1,0:T(8,128)}), f32[128,24,128]{2,1,0:T(8,128)S(1)}, u32[]{:S(2)}, u32[]{:S(2)}) async-start(f32[128,24,128]{2,1,0:T(8,128)} %pack_tiles.3), calls=%async_computation | async-start | bytes 3145728 | tf_op jit(solution)/shard_map/all_to_all | solution.py:479
  55.2 1.2 copy-start
  55.5 12.3 %copy-start.1 = (s32[128,128]{1,0:T(8,128)}, s32[128,128]{1,0:T(8,128)S(1)}, u32[]{:S(2)}) copy-start(s32[128,128]{1,0:T(8,128)S(1)} %fusion.5.target_ref) | copy-start | bytes 196612
  61.6 4.9 %collective-permute-start = (f32[4,32,128]{2,1,0:T(8,128)}, f32[4,32,128]{2,1,0:T(8,128)S(1)}, u32[]{:S(2)}, u32[]{:S(2)}) collective-permute-start(f32[4,32,128]{2,1,0:T(8,128)} %bitcast.58), channel_id=1, source_target_pairs={{0,2},{1,3},{2,4},{3,5},{4,6},{5,7},{6,0},{7,1},{8,10},{9,11},{10,... | collective-permute-start | bytes 196616 | tf_op jit(solution)/shard_map/ppermute | solution.py:504
  61.6 5.3 %collective-permute-start.1 = (f32[4,32,128]{2,1,0:T(8,128)}, f32[4,32,128]{2,1,0:T(8,128)S(1)}, u32[]{:S(2)}, u32[]{:S(2)}) collective-permute-start(f32[4,32,128]{2,1,0:T(8,128)} %bitcast.59), channel_id=1, source_target_pairs={{0,4},{1,5},{2,6},{3,7},{4,0},{5,1},{6,2},{7,3},{8,12},{9,13},{10,... | collective-permute-start | bytes 196616 | tf_op jit(solution)/shard_map/ppermute | solution.py:504
  62.6 5.1 %collective-permute-start.2 = (f32[4,32,128]{2,1,0:T(8,128)}, f32[4,32,128]{2,1,0:T(8,128)S(1)}, u32[]{:S(2)}, u32[]{:S(2)}) collective-permute-start(f32[4,32,128]{2,1,0:T(8,128)} %bitcast.60), channel_id=1, source_target_pairs={{0,6},{1,7},{2,0},{3,1},{4,2},{5,3},{6,4},{7,5},{8,14},{9,15},{10,... | collective-permute-start | bytes 196616 | tf_op jit(solution)/shard_map/ppermute | solution.py:504
  67.8 0.7 copy-start.2
  68.5 134.8 %all-to-all-start.1 = ((f32[128,144,128]{2,1,0:T(8,128)}), f32[128,144,128]{2,1,0:T(8,128)}, u32[]{:S(2)}, u32[]{:S(2)}) async-start(f32[128,144,128]{2,1,0:T(8,128)} %pack_tiles.4), calls=%async_computation.1 | async-start | bytes 18874368 | tf_op jit(solution)/shard_map/all_to_all | solution.py:479
  75.4 152.9 %all-gather.3.cloned.1.call-start = ((), (), s32[]{:S(2)}) async-start(), calls=%async_computation.4 | async-start | bytes 4456448 | tf_op jit(solution)/shard_map/all_gather | solution.py:509
  228.4 14.7 %collective-permute-start.3 = (f32[64,4,32,128]{3,2,1,0:T(8,128)}, f32[64,4,32,128]{3,2,1,0:T(8,128)}, u32[]{:S(2)}, u32[]{:S(2)}) collective-permute-start(f32[64,4,32,128]{3,2,1,0:T(8,128)} %all-gather.3.cloned.1.call-done.top_ref), channel_id=1, source_target_pairs={{0,1},{1,0},{2,3},{3,2},{4,5},{5,4},{6,7},{7,6},{8,9},{9,8},{10,11... | collective-permute-start | bytes 12582920 | tf_op jit(solution)/shard_map/ppermute | solution.py:518
  230.2 62.2 %all-to-all-start.2 = ((f32[128,64,128]{2,1,0:T(8,128)}), f32[128,64,128]{2,1,0:T(8,128)}, u32[]{:S(2)}, u32[]{:S(2)}) async-start(f32[128,64,128]{2,1,0:T(8,128)} %pack_tiles.5), calls=%async_computation.2 | async-start | bytes 8388608 | tf_op jit(solution)/shard_map/all_to_all | solution.py:479
Sparse Core Ops, SparseCore 0:
  78.4 132.6 all-gather.2

commit v6 on v5

--- a/solution.py
+++ b/solution.py
@@ -8,7 +8,7 @@
 NF = 49152
 EARLY = 8
 GROUP = 8
-CHUNKS = (72, 32)
+CHUNKS = (64, 40)
 BULK = 2**31
 HIGHEST = lax.Precision.HIGHEST
 VMEM_BYTES = 56 * 1024 * 1024
@@ -512,7 +512,7 @@
     received0, second_pack = lax.optimization_barrier((received0, second_pack))
     received1 = exchange(second_pack)
     pieces = received0.reshape(devices, CHUNKS[0], 2, lanes)
-    sums = add_pieces(targets, pieces, early, None, at, 12, BULK)
+    sums = add_pieces(targets, pieces, early, None, at, 16, BULK)
     top, sums = lax.optimization_barrier((top, sums))
     swap = [(i, i + 1 - 2 * (i % 2)) for i in range(n_col)]
     other_top = lax.ppermute(top, "col", swap)
@@ -533,7 +533,7 @@
     own_rows = jnp.pad(own_rows.reshape(top_cols, top_cols * lanes), ((0, 8 - top_cols), (0, 0)))
     received1, inverse, own_rows = lax.optimization_barrier((received1, inverse, own_rows))
     pieces = received1.reshape(devices, CHUNKS[1], 2, lanes)
-    sums = add_pieces(targets, pieces, None, sums, at + CHUNKS[0], 16, BULK)
+    sums = add_pieces(targets, pieces, None, sums, at + CHUNKS[0], 20, BULK)
 
     own = jnp.where(jnp.arange(lanes, dtype=jnp.int32)[None, :] == me, diagonal, 0.0)
     result = update_rows(

time: 423 us -> 395 us (0.934)
  waiting for transfers between devices: 155 us -> 125 us
    all_to_all x3, waiting for transfers between devices: 151 us -> 118 us  [exchange(): return lax.all_to_all(x, axes, split_axis=0, concat_axis=0, tiled=True)]
  transfers between devices with their start and end apart: 8 -> 8, of which waited for: 6 -> 7; matrix products, arithmetic and copies ran while one was open for 2% -> 2% of each run, Pallas kernels for 17% -> 18%
where the time goes in v6:
time: 395 us; the launch traced here: 393 us
  waiting for transfers between devices  125 us (32%)
  Pallas kernels  121 us (31%)
  blocking collectives  82.7 us (21%)
  starting transfers between devices  32.1 us (8%)
  between operations  14.3 us (4%)
  local copies, waits for them, and re-layouts  9.93 us (3%)
  other arithmetic  6.69 us (2%)
    all_to_all x3, waiting for transfers between devices, exchange(): return lax.all_to_all(x, axes, split_axis=0, concat_axis=0, tiled=True)  118 us
    all_to_all x1, blocking collectives, exchange(): return lax.all_to_all(x, axes, split_axis=0, concat_axis=0, tiled=True)  82.7 us
    pallas_call x2, Pallas kernels, add_pieces(): pl.pallas_call(body, grid_spec=pltpu.PrefetchScalarGridSpec(num_scalar_pr...  42.2 us
    all_to_all x3, starting transfers between devices, exchange(): return lax.all_to_all(x, axes, split_axis=0, concat_axis=0, tiled=True)  28.3 us
    pallas_call x1, Pallas kernels, factor_corner(): pl.pallas_call(body, out_shape=(shape, shape), scratch_shapes=[pltpu.VMEM...  26.2 us
    pallas_call x3, Pallas kernels, pack_tiles(): pl.pallas_call(body, grid_spec=pltpu.PrefetchScalarGridSpec(num_scalar_pr...  24.1 us
    pallas_call x1, Pallas kernels, update_rows(): pl.pallas_call(body, grid_spec=pltpu.PrefetchScalarGridSpec(num_scalar_pr...  18.2 us
  transfers between devices with their start and end apart: 8, of which 7 were waited for; matrix products, arithmetic and copies ran while one was open for 2% of the time, Pallas kernels for 18%

profile of v6, /device:TPU:1, one launch (start us, length us, event | category | flops | bytes accessed | tf_op | source)
XLA Modules:
  0.0 392.6 jit_solution(1104549606307932397)
XLA Ops:
  6.5 0.9 fusion.11
  7.5 0.9 fusion.15
  11.3 1.2 convolution_bitcast_fusion
  12.4 1.8 copy.22
  15.0 3.9 pack_tiles.3
  18.8 11.5 %all-to-all-start = ((f32[128,24,128]{2,1,0:T(8,128)}), f32[128,24,128]{2,1,0:T(8,128)S(1)}, u32[]{:S(2)}, u32[]{:S(2)}) async-start(f32[128,24,128]{2,1,0:T(8,128)} %pack_tiles.3), calls=%async_computation | async-start | bytes 3145728 | tf_op jit(solution)/shard_map/all_to_all | solution.py:479
  30.4 11.7 %pack_tiles.4 = f32[128,128,128]{2,1,0:T(8,128)} custom-call(s32[112]{0:T(128)} %get-tuple-element.32.order_ref, f32[112,256,128]{2,1,0:T(8,128)} %refs_7_.5, f32[112,256,128]{2,1,0:T(8,128)} %refs_7_.5, f32[112,256,128]{2,1,0:T(8,128)} %refs_7_.5, f32[112,256,128]{2,1,0:T(8,128)} %refs_7_.5, f32[112,256,128]{2,1,0:T(8,128)} %refs_7_.5, ...), custom_call_target="tpu_custom_call" | custom-call | tf_op jit(solution)/shard_map/pack_tiles/pallas_call | solution.py:51
  42.0 13.2 %all-to-all-done = f32[128,24,128]{2,1,0:T(8,128)S(1)} async-done(((f32[128,24,128]{2,1,0:T(8,128)}), f32[128,24,128]{2,1,0:T(8,128)S(1)}, u32[]{:S(2)}, u32[]{:S(2)}) %all-to-all-start) | async-done | bytes 1572896 | tf_op jit(solution)/shard_map/all_to_all | solution.py:479
  55.6 0.9 fusion.4.spot_ref
  56.5 5.3 %add_top.1 = f32[64,2,128]{2,1,0:T(2,128)} custom-call(s32[128,8]{1,0:T(8,128)} %fusion.4.spot_ref, f32[128,12,2,128]{3,2,1,0:T(2,128)} %bitcast.51), custom_call_target="tpu_custom_call" | custom-call | tf_op jit(solution)/shard_map/add_top/pallas_call | solution.py:133
  61.7 1.0 collective-permute-start.1
  62.7 1.7 collective-permute-start.2
  64.4 0.9 constant_dynamic-update-slice_fusion
  65.3 1.4 collective-permute-done
  67.1 0.8 collective-permute-done.2
  68.5 7.0 %all-to-all-start.1 = ((f32[128,128,128]{2,1,0:T(8,128)}), f32[128,128,128]{2,1,0:T(8,128)}, u32[]{:S(2)}, u32[]{:S(2)}) async-start(f32[128,128,128]{2,1,0:T(8,128)} %pack_tiles.4), calls=%async_computation.1 | async-start | bytes 16777216 | tf_op jit(solution)/shard_map/all_to_all | solution.py:479
  76.3 8.5 %pack_tiles.5 = f32[128,80,128]{2,1,0:T(8,128)} custom-call(s32[112]{0:T(128)} %get-tuple-element.32.order_ref, f32[112,256,128]{2,1,0:T(8,128)} %refs_7_.5, f32[112,256,128]{2,1,0:T(8,128)} %refs_7_.5, f32[112,256,128]{2,1,0:T(8,128)} %refs_7_.5, f32[112,256,128]{2,1,0:T(8,128)} %refs_7_.5, f32[112,256,128]{2,1,0:T(8,128)} %refs_7_.5, ...), custom_call_target="tpu_custom_call" | custom-call | tf_op jit(solution)/shard_map/pack_tiles/pallas_call | solution.py:51
  84.9 102.6 %all-to-all-done.1 = f32[128,128,128]{2,1,0:T(8,128)} async-done(((f32[128,128,128]{2,1,0:T(8,128)}), f32[128,128,128]{2,1,0:T(8,128)}, u32[]{:S(2)}, u32[]{:S(2)}) %all-to-all-start.1) | async-done | bytes 8388640 | tf_op jit(solution)/shard_map/all_to_all | solution.py:479
  187.5 9.7 %all-to-all-start.2 = ((f32[128,80,128]{2,1,0:T(8,128)}), f32[128,80,128]{2,1,0:T(8,128)}, u32[]{:S(2)}, u32[]{:S(2)}) async-start(f32[128,80,128]{2,1,0:T(8,128)} %pack_tiles.5), calls=%async_computation.2 | async-start | bytes 10485760 | tf_op jit(solution)/shard_map/all_to_all | solution.py:479
  197.2 23.8 %add_pieces.2.refs_0_ = f32[6144,2,128]{2,1,0:T(2,128)} custom-call(s32[128,128]{1,0:T(8,128)} %copy-done.1, f32[128,64,2,128]{3,2,1,0:T(2,128)} %bitcast.13.pieces_ref, f32[128,12,2,128]{3,2,1,0:T(2,128)} %bitcast.52), custom_call_target="tpu_custom_call" | custom-call | flops 2147483648 | bytes 2147483648 | tf_op jit(solution)/shard_map/add_pieces/pallas_call | solution.py:98
  221.0 1.1 collective-permute-start.3
  224.3 1.3 slice.27
  225.6 3.7 collective-permute-done.3.other_ref
  229.3 1.3 slice.28
  230.5 1.2 bitcast_select_fusion.corner_ref
  231.7 26.2 %factor_corner.1 = (f32[512,512]{1,0:T(8,128)}, f32[512,512]{1,0:T(8,128)}) custom-call(f32[128,16,128]{2,1,0:T(8,128)} %bitcast_select_fusion.corner_ref, f32[8,128]{1,0:T(8,128)} %slice.29.diag_ref), custom_call_target="tpu_custom_call" | custom-call | tf_op jit(solution)/shard_map/factor_corner/pallas_call | solution.py:261
  257.9 0.8 constant_dynamic-slice_fusion
  259.4 1.9 all-to-all-done.2
  261.2 18.4 %add_pieces.3 = f32[6144,2,128]{2,1,0:T(2,128)} custom-call(s32[128,128]{1,0:T(8,128)} %copy-done.1, f32[128,40,2,128]{3,2,1,0:T(2,128)} %bitcast.23.pieces_ref, f32[6144,2,128]{2,1,0:T(2,128)} %add_pieces.2.refs_0_), custom_call_target="tpu_custom_call" | custom-call | flops 2147483648 | bytes 2147483648 | tf_op jit(solution)/shard_map/add_pieces/pallas_call | solution.py:98
  279.7 18.2 %update_rows.1 = f32[16,8,96,128]{3,2,1,0:T(8,128)} custom-call(s32[1]{0:T(128)} %bitcast.core_ref, f32[2,8,2,384,128]{4,3,2,1,0:T(8,128)} %bitcast.46, f32[2,8,2,384,128]{4,3,2,1,0:T(8,128)} %bitcast.47, f32[64,4,32,128]{3,2,1,0:T(8,128)} %all-gather.3.cloned.1.call-done.top_ref, f32[64,4,32,128]{3,2,1,0:T(8,128)} %collective-permute-done.3.other_ref, ...), custom_call_target="tpu_custom_call" | custom-call | tf_op jit(solution)/shard_map/update_rows/pallas_call | solution.py:373
  297.9 82.7 %all_to_all.20 = f32[128,96,128]{2,1,0:T(8,128)} all-to-all(f32[128,96,128]{2,1,0:T(8,128)} %bitcast.54), channel_id=1, replica_groups=mesh['row'=16,'col'=8] {'row','col'}, dimensions={0} | all-to-all | bytes 12582912 | tf_op jit(solution)/shard_map/all_to_all | solution.py:479
  380.6 5.1 %place_rows.1 = f32[24,128,4,128]{3,2,1,0:T(4,128)} custom-call(f32[128,24,4,128]{3,2,1,0:T(4,128)} %bitcast.53), custom_call_target="tpu_custom_call" | custom-call | tf_op jit(solution)/shard_map/place_rows/pallas_call | solution.py:416
  (40 shorter events, 7.8 us)
Async XLA Ops:
  18.8 36.4 %all-to-all-start = ((f32[128,24,128]{2,1,0:T(8,128)}), f32[128,24,128]{2,1,0:T(8,128)S(1)}, u32[]{:S(2)}, u32[]{:S(2)}) async-start(f32[128,24,128]{2,1,0:T(8,128)} %pack_tiles.3), calls=%async_computation | async-start | bytes 3145728 | tf_op jit(solution)/shard_map/all_to_all | solution.py:479
  55.2 1.2 copy-start
  55.6 12.3 %copy-start.1 = (s32[128,128]{1,0:T(8,128)}, s32[128,128]{1,0:T(8,128)S(1)}, u32[]{:S(2)}) copy-start(s32[128,128]{1,0:T(8,128)S(1)} %fusion.5.target_ref) | copy-start | bytes 196612
  61.7 4.9 %collective-permute-start = (f32[4,32,128]{2,1,0:T(8,128)}, f32[4,32,128]{2,1,0:T(8,128)S(1)}, u32[]{:S(2)}, u32[]{:S(2)}) collective-permute-start(f32[4,32,128]{2,1,0:T(8,128)} %bitcast.58), channel_id=1, source_target_pairs={{0,2},{1,3},{2,4},{3,5},{4,6},{5,7},{6,0},{7,1},{8,10},{9,11},{10,... | collective-permute-start | bytes 196616 | tf_op jit(solution)/shard_map/ppermute | solution.py:504
  61.7 5.3 %collective-permute-start.1 = (f32[4,32,128]{2,1,0:T(8,128)}, f32[4,32,128]{2,1,0:T(8,128)S(1)}, u32[]{:S(2)}, u32[]{:S(2)}) collective-permute-start(f32[4,32,128]{2,1,0:T(8,128)} %bitcast.59), channel_id=1, source_target_pairs={{0,4},{1,5},{2,6},{3,7},{4,0},{5,1},{6,2},{7,3},{8,12},{9,13},{10,... | collective-permute-start | bytes 196616 | tf_op jit(solution)/shard_map/ppermute | solution.py:504
  62.7 5.1 %collective-permute-start.2 = (f32[4,32,128]{2,1,0:T(8,128)}, f32[4,32,128]{2,1,0:T(8,128)S(1)}, u32[]{:S(2)}, u32[]{:S(2)}) collective-permute-start(f32[4,32,128]{2,1,0:T(8,128)} %bitcast.60), channel_id=1, source_target_pairs={{0,6},{1,7},{2,0},{3,1},{4,2},{5,3},{6,4},{7,5},{8,14},{9,15},{10,... | collective-permute-start | bytes 196616 | tf_op jit(solution)/shard_map/ppermute | solution.py:504
  67.9 0.7 copy-start.2
  68.5 118.9 %all-to-all-start.1 = ((f32[128,128,128]{2,1,0:T(8,128)}), f32[128,128,128]{2,1,0:T(8,128)}, u32[]{:S(2)}, u32[]{:S(2)}) async-start(f32[128,128,128]{2,1,0:T(8,128)} %pack_tiles.4), calls=%async_computation.1 | async-start | bytes 16777216 | tf_op jit(solution)/shard_map/all_to_all | solution.py:479
  75.6 145.4 %all-gather.3.cloned.1.call-start = ((), (), s32[]{:S(2)}) async-start(), calls=%async_computation.4 | async-start | bytes 4456448 | tf_op jit(solution)/shard_map/all_gather | solution.py:509
  187.5 73.8 %all-to-all-start.2 = ((f32[128,80,128]{2,1,0:T(8,128)}), f32[128,80,128]{2,1,0:T(8,128)}, u32[]{:S(2)}, u32[]{:S(2)}) async-start(f32[128,80,128]{2,1,0:T(8,128)} %pack_tiles.5), calls=%async_computation.2 | async-start | bytes 10485760 | tf_op jit(solution)/shard_map/all_to_all | solution.py:479
  221.0 8.3 %collective-permute-start.3 = (f32[64,4,32,128]{3,2,1,0:T(8,128)}, f32[64,4,32,128]{3,2,1,0:T(8,128)}, u32[]{:S(2)}, u32[]{:S(2)}) collective-permute-start(f32[64,4,32,128]{3,2,1,0:T(8,128)} %all-gather.3.cloned.1.call-done.top_ref), channel_id=1, source_target_pairs={{0,1},{1,0},{2,3},{3,2},{4,5},{5,4},{6,7},{7,6},{8,9},{9,8},{10,11... | collective-permute-start | bytes 12582920 | tf_op jit(solution)/shard_map/ppermute | solution.py:518
Sparse Core Ops, SparseCore 0:
  78.6 119.2 all-gather.2

commit v7 on v6

--- a/solution.py
+++ b/solution.py
@@ -66,7 +66,7 @@
 def add_pieces(targets, pieces, early, sums, first, window, weight):
     sources, count, two, lanes = pieces.shape
     n_sums = 6144
-    per_step = 8
+    per_step = 32
     fresh = sums is None
 
     def body(target_ref, pieces_ref, *refs):

time: 395 us -> 390 us (0.987)
  Pallas kernels: 121 us -> 117 us
where the time goes in v7:
time: 390 us; the launch traced here: 389 us
  waiting for transfers between devices  124 us (32%)
  Pallas kernels  117 us (30%)
  blocking collectives  82.7 us (21%)
  starting transfers between devices  32.3 us (8%)
  between operations  14.3 us (4%)
  local copies, waits for them, and re-layouts  9.93 us (3%)
  other arithmetic  6.69 us (2%)
    all_to_all x3, waiting for transfers between devices, exchange(): return lax.all_to_all(x, axes, split_axis=0, concat_axis=0, tiled=True)  118 us
    all_to_all x1, blocking collectives, exchange(): return lax.all_to_all(x, axes, split_axis=0, concat_axis=0, tiled=True)  82.7 us
    pallas_call x2, Pallas kernels, add_pieces(): pl.pallas_call(body, grid_spec=pltpu.PrefetchScalarGridSpec(num_scalar_pr...  38.4 us
    all_to_all x3, starting transfers between devices, exchange(): return lax.all_to_all(x, axes, split_axis=0, concat_axis=0, tiled=True)  28.3 us
    pallas_call x1, Pallas kernels, factor_corner(): pl.pallas_call(body, out_shape=(shape, shape), scratch_shapes=[pltpu.VMEM...  26 us
    pallas_call x3, Pallas kernels, pack_tiles(): pl.pallas_call(body, grid_spec=pltpu.PrefetchScalarGridSpec(num_scalar_pr...  24.1 us
    pallas_call x1, Pallas kernels, update_rows(): pl.pallas_call(body, grid_spec=pltpu.PrefetchScalarGridSpec(num_scalar_pr...  18.2 us
  transfers between devices with their start and end apart: 8, of which 7 were waited for; matrix products, arithmetic and copies ran while one was open for 2% of the time, Pallas kernels for 18%

profile of v7, /device:TPU:1, one launch (start us, length us, event | category | flops | bytes accessed | tf_op | source)
XLA Modules:
  0.0 388.6 jit_solution(969330722521404166)
XLA Ops:
  6.5 0.9 fusion.11
  7.5 0.9 fusion.15
  11.3 1.2 convolution_bitcast_fusion
  12.4 1.8 copy.22
  15.0 3.9 pack_tiles.3
  18.8 11.5 %all-to-all-start = ((f32[128,24,128]{2,1,0:T(8,128)}), f32[128,24,128]{2,1,0:T(8,128)S(1)}, u32[]{:S(2)}, u32[]{:S(2)}) async-start(f32[128,24,128]{2,1,0:T(8,128)} %pack_tiles.3), calls=%async_computation | async-start | bytes 3145728 | tf_op jit(solution)/shard_map/all_to_all | solution.py:479
  30.4 11.7 %pack_tiles.4 = f32[128,128,128]{2,1,0:T(8,128)} custom-call(s32[112]{0:T(128)} %get-tuple-element.32.order_ref, f32[112,256,128]{2,1,0:T(8,128)} %refs_7_.5, f32[112,256,128]{2,1,0:T(8,128)} %refs_7_.5, f32[112,256,128]{2,1,0:T(8,128)} %refs_7_.5, f32[112,256,128]{2,1,0:T(8,128)} %refs_7_.5, f32[112,256,128]{2,1,0:T(8,128)} %refs_7_.5, ...), custom_call_target="tpu_custom_call" | custom-call | tf_op jit(solution)/shard_map/pack_tiles/pallas_call | solution.py:51
  42.0 13.2 %all-to-all-done = f32[128,24,128]{2,1,0:T(8,128)S(1)} async-done(((f32[128,24,128]{2,1,0:T(8,128)}), f32[128,24,128]{2,1,0:T(8,128)S(1)}, u32[]{:S(2)}, u32[]{:S(2)}) %all-to-all-start) | async-done | bytes 1572896 | tf_op jit(solution)/shard_map/all_to_all | solution.py:479
  55.6 0.9 fusion.4.spot_ref
  56.5 5.3 %add_top.1 = f32[64,2,128]{2,1,0:T(2,128)} custom-call(s32[128,8]{1,0:T(8,128)} %fusion.4.spot_ref, f32[128,12,2,128]{3,2,1,0:T(2,128)} %bitcast.51), custom_call_target="tpu_custom_call" | custom-call | tf_op jit(solution)/shard_map/add_top/pallas_call | solution.py:133
  61.7 1.0 collective-permute-start.1
  62.7 1.7 collective-permute-start.2
  64.4 0.9 constant_dynamic-update-slice_fusion
  65.3 1.4 collective-permute-done
  67.1 0.8 collective-permute-done.2
  68.5 7.0 %all-to-all-start.1 = ((f32[128,128,128]{2,1,0:T(8,128)}), f32[128,128,128]{2,1,0:T(8,128)}, u32[]{:S(2)}, u32[]{:S(2)}) async-start(f32[128,128,128]{2,1,0:T(8,128)} %pack_tiles.4), calls=%async_computation.1 | async-start | bytes 16777216 | tf_op jit(solution)/shard_map/all_to_all | solution.py:479
  76.3 8.5 %pack_tiles.5 = f32[128,80,128]{2,1,0:T(8,128)} custom-call(s32[112]{0:T(128)} %get-tuple-element.32.order_ref, f32[112,256,128]{2,1,0:T(8,128)} %refs_7_.5, f32[112,256,128]{2,1,0:T(8,128)} %refs_7_.5, f32[112,256,128]{2,1,0:T(8,128)} %refs_7_.5, f32[112,256,128]{2,1,0:T(8,128)} %refs_7_.5, f32[112,256,128]{2,1,0:T(8,128)} %refs_7_.5, ...), custom_call_target="tpu_custom_call" | custom-call | tf_op jit(solution)/shard_map/pack_tiles/pallas_call | solution.py:51
  84.9 102.6 %all-to-all-done.1 = f32[128,128,128]{2,1,0:T(8,128)} async-done(((f32[128,128,128]{2,1,0:T(8,128)}), f32[128,128,128]{2,1,0:T(8,128)}, u32[]{:S(2)}, u32[]{:S(2)}) %all-to-all-start.1) | async-done | bytes 8388640 | tf_op jit(solution)/shard_map/all_to_all | solution.py:479
  187.5 9.8 %all-to-all-start.2 = ((f32[128,80,128]{2,1,0:T(8,128)}), f32[128,80,128]{2,1,0:T(8,128)}, u32[]{:S(2)}, u32[]{:S(2)}) async-start(f32[128,80,128]{2,1,0:T(8,128)} %pack_tiles.5), calls=%async_computation.2 | async-start | bytes 10485760 | tf_op jit(solution)/shard_map/all_to_all | solution.py:479
  197.2 24.0 %add_pieces.2.refs_0_ = f32[6144,2,128]{2,1,0:T(2,128)} custom-call(s32[128,128]{1,0:T(8,128)} %copy-done.1, f32[128,64,2,128]{3,2,1,0:T(2,128)} %bitcast.13.pieces_ref, f32[128,12,2,128]{3,2,1,0:T(2,128)} %bitcast.52), custom_call_target="tpu_custom_call" | custom-call | flops 2147483648 | bytes 2147483648 | tf_op jit(solution)/shard_map/add_pieces/pallas_call | solution.py:98
  221.2 1.3 collective-permute-start.3
  224.7 1.3 slice.27
  226.0 3.7 collective-permute-done.3.other_ref
  229.6 1.3 slice.28
  230.9 1.2 bitcast_select_fusion.corner_ref
  232.1 26.0 %factor_corner.1 = (f32[512,512]{1,0:T(8,128)}, f32[512,512]{1,0:T(8,128)}) custom-call(f32[128,16,128]{2,1,0:T(8,128)} %bitcast_select_fusion.corner_ref, f32[8,128]{1,0:T(8,128)} %slice.29.diag_ref), custom_call_target="tpu_custom_call" | custom-call | tf_op jit(solution)/shard_map/factor_corner/pallas_call | solution.py:261
  258.1 0.8 constant_dynamic-slice_fusion
  259.5 1.7 all-to-all-done.2
  261.2 14.5 %add_pieces.3 = f32[6144,2,128]{2,1,0:T(2,128)} custom-call(s32[128,128]{1,0:T(8,128)} %copy-done.1, f32[128,40,2,128]{3,2,1,0:T(2,128)} %bitcast.23.pieces_ref, f32[6144,2,128]{2,1,0:T(2,128)} %add_pieces.2.refs_0_), custom_call_target="tpu_custom_call" | custom-call | flops 2147483648 | bytes 2147483648 | tf_op jit(solution)/shard_map/add_pieces/pallas_call | solution.py:98
  275.7 18.2 %update_rows.1 = f32[16,8,96,128]{3,2,1,0:T(8,128)} custom-call(s32[1]{0:T(128)} %bitcast.core_ref, f32[2,8,2,384,128]{4,3,2,1,0:T(8,128)} %bitcast.46, f32[2,8,2,384,128]{4,3,2,1,0:T(8,128)} %bitcast.47, f32[64,4,32,128]{3,2,1,0:T(8,128)} %all-gather.3.cloned.1.call-done.top_ref, f32[64,4,32,128]{3,2,1,0:T(8,128)} %collective-permute-done.3.other_ref, ...), custom_call_target="tpu_custom_call" | custom-call | tf_op jit(solution)/shard_map/update_rows/pallas_call | solution.py:373
  293.9 82.7 %all_to_all.20 = f32[128,96,128]{2,1,0:T(8,128)} all-to-all(f32[128,96,128]{2,1,0:T(8,128)} %bitcast.54), channel_id=1, replica_groups=mesh['row'=16,'col'=8] {'row','col'}, dimensions={0} | all-to-all | bytes 12582912 | tf_op jit(solution)/shard_map/all_to_all | solution.py:479
  376.6 5.1 %place_rows.1 = f32[24,128,4,128]{3,2,1,0:T(4,128)} custom-call(f32[128,24,4,128]{3,2,1,0:T(4,128)} %bitcast.53), custom_call_target="tpu_custom_call" | custom-call | tf_op jit(solution)/shard_map/place_rows/pallas_call | solution.py:416
  (40 shorter events, 7.8 us)
Async XLA Ops:
  18.8 36.4 %all-to-all-start = ((f32[128,24,128]{2,1,0:T(8,128)}), f32[128,24,128]{2,1,0:T(8,128)S(1)}, u32[]{:S(2)}, u32[]{:S(2)}) async-start(f32[128,24,128]{2,1,0:T(8,128)} %pack_tiles.3), calls=%async_computation | async-start | bytes 3145728 | tf_op jit(solution)/shard_map/all_to_all | solution.py:479
  55.2 1.2 copy-start
  55.6 12.3 %copy-start.1 = (s32[128,128]{1,0:T(8,128)}, s32[128,128]{1,0:T(8,128)S(1)}, u32[]{:S(2)}) copy-start(s32[128,128]{1,0:T(8,128)S(1)} %fusion.5.target_ref) | copy-start | bytes 196612
  61.7 4.9 %collective-permute-start = (f32[4,32,128]{2,1,0:T(8,128)}, f32[4,32,128]{2,1,0:T(8,128)S(1)}, u32[]{:S(2)}, u32[]{:S(2)}) collective-permute-start(f32[4,32,128]{2,1,0:T(8,128)} %bitcast.58), channel_id=1, source_target_pairs={{0,2},{1,3},{2,4},{3,5},{4,6},{5,7},{6,0},{7,1},{8,10},{9,11},{10,... | collective-permute-start | bytes 196616 | tf_op jit(solution)/shard_map/ppermute | solution.py:504
  61.7 5.3 %collective-permute-start.1 = (f32[4,32,128]{2,1,0:T(8,128)}, f32[4,32,128]{2,1,0:T(8,128)S(1)}, u32[]{:S(2)}, u32[]{:S(2)}) collective-permute-start(f32[4,32,128]{2,1,0:T(8,128)} %bitcast.59), channel_id=1, source_target_pairs={{0,4},{1,5},{2,6},{3,7},{4,0},{5,1},{6,2},{7,3},{8,12},{9,13},{10,... | collective-permute-start | bytes 196616 | tf_op jit(solution)/shard_map/ppermute | solution.py:504
  62.7 5.1 %collective-permute-start.2 = (f32[4,32,128]{2,1,0:T(8,128)}, f32[4,32,128]{2,1,0:T(8,128)S(1)}, u32[]{:S(2)}, u32[]{:S(2)}) collective-permute-start(f32[4,32,128]{2,1,0:T(8,128)} %bitcast.60), channel_id=1, source_target_pairs={{0,6},{1,7},{2,0},{3,1},{4,2},{5,3},{6,4},{7,5},{8,14},{9,15},{10,... | collective-permute-start | bytes 196616 | tf_op jit(solution)/shard_map/ppermute | solution.py:504
  67.9 0.7 copy-start.2
  68.5 118.9 %all-to-all-start.1 = ((f32[128,128,128]{2,1,0:T(8,128)}), f32[128,128,128]{2,1,0:T(8,128)}, u32[]{:S(2)}, u32[]{:S(2)}) async-start(f32[128,128,128]{2,1,0:T(8,128)} %pack_tiles.4), calls=%async_computation.1 | async-start | bytes 16777216 | tf_op jit(solution)/shard_map/all_to_all | solution.py:479
  75.6 145.6 %all-gather.3.cloned.1.call-start = ((), (), s32[]{:S(2)}) async-start(), calls=%async_computation.4 | async-start | bytes 4456448 | tf_op jit(solution)/shard_map/all_gather | solution.py:509
  187.5 73.8 %all-to-all-start.2 = ((f32[128,80,128]{2,1,0:T(8,128)}), f32[128,80,128]{2,1,0:T(8,128)}, u32[]{:S(2)}, u32[]{:S(2)}) async-start(f32[128,80,128]{2,1,0:T(8,128)} %pack_tiles.5), calls=%async_computation.2 | async-start | bytes 10485760 | tf_op jit(solution)/shard_map/all_to_all | solution.py:479
  221.2 8.4 %collective-permute-start.3 = (f32[64,4,32,128]{3,2,1,0:T(8,128)}, f32[64,4,32,128]{3,2,1,0:T(8,128)}, u32[]{:S(2)}, u32[]{:S(2)}) collective-permute-start(f32[64,4,32,128]{3,2,1,0:T(8,128)} %all-gather.3.cloned.1.call-done.top_ref), channel_id=1, source_target_pairs={{0,1},{1,0},{2,3},{3,2},{4,5},{5,4},{6,7},{7,6},{8,9},{9,8},{10,11... | collective-permute-start | bytes 12582920 | tf_op jit(solution)/shard_map/ppermute | solution.py:518
Sparse Core Ops, SparseCore 0:
  78.6 119.2 all-gather.2
